TPU v7x, 512 devices: a whole 4x4x16 slice. The times are simulated.
512 devices in a mesh: dp: 16 (over z), tensor: 32 (over x, y, core).
Axes of the slice: x: 4, y: 4, z: 16, core: 2. Of those that a mesh axis runs over, the one named last changes fastest.
Arguments:
- hidden: bfloat16 [14336, 4096], P('dp', 'tensor')
- gain: bfloat16 [4096], P('tensor'), may hold values from 0.5 to 1.5
- head_weight: bfloat16 [4096, 32000], P('dp', 'tensor')
- targets: int32 [14336], P('dp'), may hold values from 0 to 31999
- seq_ids: int32 [14336], P(('dp', 'tensor')), may hold values from 0 to 63, never falling along the last dimension, each value on 1 to 1792 neighbouring positions
- live: int32 [14336], P(('dp', 'tensor')), may hold values 0 or 1
Outputs:
- logprob: float32 [14336], P(('dp', 'tensor'))
- entropy: float32 [14336], P(('dp', 'tensor'))
- seq_mean: float32 [64], replicated
Inputs may be any that keep to these rules, and one draw needn't show every extreme that they name: `seq_ids`: sequence numbers never fall along the tokens; each sequence has 1 to 1792 tokens, one exactly 1792.
All inputs are finite; a program needn't handle non-finite values. No bound on the sum of `live` on one device may be relied on, other than what follows from the above.
Results may differ from a plain program's by a relative error of at most 0.0015.
Values may be sent and summed in bfloat16 or wider, within the bound.
No kernel may reach another device: no remote copies, remote signals or barrier semaphores. Data moves between devices by JAX's collectives and lax.ppermute only.
A program may use at most 64 MiB of HBM per device.

v0:
```python
import jax
import jax.numpy as jnp
from jax import lax
from jax.sharding import PartitionSpec as P

SEQ_DEV = 4


def body(hidden, gain, head_weight, targets, seq_ids, live):
    shards = lax.axis_size("tensor")
    rank = lax.axis_index("tensor")
    tok_rows = hidden.shape[0]
    share = tok_rows // shards
    vocab_dev = head_weight.shape[1]
    whole, gains = (
        lax.all_gather(hidden, "tensor", axis=1, tiled=True),
        lax.all_gather(gain, "tensor", axis=0, tiled=True),
    )
    values = whole.astype(jnp.float32)
    meansq = jnp.mean(values * values, axis=-1, keepdims=True)
    normed = (values * lax.rsqrt(meansq + 1e-05) * gains.astype(jnp.float32)).astype(jnp.bfloat16)
    scores = jnp.dot(
        normed,
        lax.all_gather(head_weight, "dp", axis=0, tiled=True),
        preferred_element_type=jnp.float32,
    )
    top = jnp.max(scores, axis=-1)
    shifted = scores - top[:, None]
    expo = jnp.exp(shifted)
    total = jnp.sum(expo, axis=-1)
    spread = jnp.sum(expo * shifted, axis=-1)
    local_ids = targets - rank * vocab_dev
    inside = (local_ids >= 0) & (local_ids < vocab_dev)
    picked = jnp.take_along_axis(scores, jnp.clip(local_ids, 0, vocab_dev - 1)[:, None], axis=1)[
        :, 0
    ]
    target_score = jnp.where(inside, picked, 0.0)
    offset = rank * share
    best = lax.pmax(top, "tensor")
    scale = jnp.exp(top - best)
    sums = lax.psum(
        (total * scale, (spread + (top - best) * total) * scale, target_score), "tensor"
    )
    g_top = lax.dynamic_slice_in_dim(best, offset, share, 0)
    g_total = lax.dynamic_slice_in_dim(sums[0], offset, share, 0)
    g_spread = lax.dynamic_slice_in_dim(sums[1], offset, share, 0)
    g_target = lax.dynamic_slice_in_dim(sums[2], offset, share, 0)
    weight = live.astype(jnp.float32)
    log_total = jnp.log(g_total)
    logprob = (g_target - g_top - log_total) * weight
    entropy = (log_total - g_spread / g_total) * weight
    seq_count = SEQ_DEV * lax.axis_size("dp")
    member = (seq_ids[:, None] == jnp.arange(seq_count)[None, :]).astype(jnp.float32)
    seq_sums = jnp.sum(member * logprob[:, None], axis=0)
    seq_live = jnp.sum(member * weight[:, None], axis=0)
    seq_sums, seq_live = lax.psum((seq_sums, seq_live), ("dp", "tensor"))
    seq_mean = seq_sums / jnp.maximum(seq_live, 1.0)
    return (logprob, entropy, seq_mean)


def solution(mesh):
    placed = (
        P("dp", "tensor"),
        P("tensor"),
        P("dp", "tensor"),
        P("dp"),
        P(("dp", "tensor")),
        P(("dp", "tensor")),
    )
    return jax.shard_map(
        body,
        mesh=mesh,
        in_specs=placed,
        out_specs=(P(("dp", "tensor")), P(("dp", "tensor")), P()),
        check_vma=False,
    )
```

profile of v0, /device:TPU:1, one launch (start us, length us, event | category | flops | bytes accessed | tf_op | source)
XLA Modules:
  0.0 560.1 jit_solution(8000703077066795527)
XLA Ops:
  7.2 0.0 all-gather.4.cloned.1.call-start
  7.2 0.7 all-gather.4.cloned.1.call-update
  7.9 0.0 all-gather.6.cloned.1.call-start
  7.9 0.7 all-gather.6.cloned.1.call-update
  8.7 24.1 %all-gather = bf16[32,1,128]{2,1,0:T(2,128)(2,1)S(1)} all-gather(bf16[1,1,128]{2,1,0:T(2,128)(2,1)} %bitcast.6), channel_id=1, replica_groups=mesh['dp'=16,'tensor'=32] {'tensor'}, dimensions={0}, use_global_device_ids=true | all-gather | bytes 8448 | tf_op jit(solution)/shard_map/all_gather | solution.py:17
  32.8 0.7 compare_select_fusion
  33.5 0.7 convert_element_type.16
  34.2 54.0 %all-gather.4.cloned.1.call-done = bf16[896,4096]{1,0:T(8,128)(2,1)} async-done(((bf16[896,128]{1,0:T(8,128)(2,1)}), bf16[896,4096]{1,0:T(8,128)(2,1)}) %all-gather.4.cloned.1.call-update) | async-done | bytes 7340048 | tf_op jit(solution)/shard_map/all_gather | solution.py:16
  88.3 4.6 fusion
  92.8 114.5 %all-gather.6.cloned.1.call-done = bf16[4096,1000]{0,1:T(8,128)(2,1)} async-done(((bf16[256,1000]{0,1:T(8,128)(2,1)}), bf16[4096,1000]{0,1:T(8,128)(2,1)}) %all-gather.6.cloned.1.call-update) | async-done | bytes 8192016 | tf_op jit(solution)/shard_map/all_gather | solution.py:24
  207.3 14.7 %fusion.12 = (f32[896]{0:T(1024)S(1)}, f32[896,1000]{0,1:T(8,128)}) fusion(bf16[4096,1000]{0,1:T(8,128)(2,1)} %all-gather.6.cloned.1.call-done, bf16[896,4096]{1,0:T(8,128)(2,1)} %all-gather.4.cloned.1.call-done, f32[4096]{0:T(1024)S(1)} %bitcast.5, f32[896]{0:T(1024)S(1)} %add_rsqrt_fusion), kind=kOutput, calls=%fused_computation.30 | convolution fusion | flops 7355607040 | bytes 19139584 | tf_op jit(solution)/shard_map/dot_general | solution.py:22
  222.1 0.0 copy-start
  222.1 0.0 copy-start.3
  222.1 0.0 copy-start.2
  222.1 73.2 %pmax.7 = f32[896]{0:T(1024)S(1)} all-reduce(f32[896]{0:T(1024)S(1)} %get-tuple-element.16), channel_id=1, replica_groups=mesh['dp'=16,'tensor'=32] {'tensor'}, use_global_device_ids=true, to_apply=%region_3.0 | all-reduce | flops 896 | bytes 7168 | tf_op jit(solution)/shard_map/pmax | solution.py:39
  295.2 2.7 fusion.7
  298.0 31.9 %gather_fusion = f32[896]{0:T(1024)S(1)} fusion(f32[896,1000]{0,1:T(8,128)} %get-tuple-element.17, s32[896]{0:T(1024)S(1)} %fusion.11), kind=kCustom, calls=%fused_computation | custom fusion | bytes 14336 | tf_op jit(solution)/shard_map/jit(take_along_axis)/gather | solution.py:34
  329.9 0.0 copy-done
  329.9 119.4 %all-reduce.1 = (f32[896]{0:T(1024)S(1)}, f32[896]{0:T(1024)S(1)}, f32[896]{0:T(1024)S(1)}) all-reduce(f32[896]{0:T(1024)S(1)} %select_select_fusion, f32[896]{0:T(1024)S(1)} %get-tuple-element.13, f32[896]{0:T(1024)S(1)} %get-tuple-element.12), channel_id=1, replica_groups=mesh['dp'=16,'tensor'=32] {'tensor'}, use_global_device_ids=true, to_apply=%region_1.0 | all-reduce | flops 2688 | bytes 21504 | tf_op jit(solution)/shard_map/psum | solution.py:41
  449.4 0.0 copy-done.3
  449.4 0.6 subtract_multiply_fusion
  450.0 0.0 copy-start.1
  450.0 0.0 copy-done.2
  450.0 0.1 select_reduce_fusion
  450.1 102.6 %all-reduce = (f32[64]{0:T(128)S(1)}, f32[64]{0:T(128)S(1)}) all-reduce(f32[64]{0:T(128)S(1)} %get-tuple-element.6, f32[64]{0:T(128)S(1)} %get-tuple-element.5), channel_id=1, replica_groups=mesh['dp'=16,'tensor'=32] {'dp','tensor'}, use_global_device_ids=true, to_apply=%region_9.10 | all-reduce | flops 128 | bytes 1024 | tf_op jit(solution)/shard_map/psum | solution.py:56
  552.7 0.5 maximum_divide_fusion
  553.3 0.0 copy-done.1
  (8 shorter events, 0.1 us)
Async XLA Ops:
  7.2 81.1 %all-gather.4.cloned.1.call-start = ((), (), s32[]{:S(2)}) async-start(), calls=%async_computation | async-start | bytes 7569408 | tf_op jit(solution)/shard_map/all_gather | solution.py:16
  7.9 199.4 %all-gather.6.cloned.1.call-start = ((), (), s32[]{:S(2)}) async-start(), calls=%async_computation.1 | async-start | bytes 8704000 | tf_op jit(solution)/shard_map/all_gather | solution.py:24
  222.1 107.9 %copy-start = (s32[896]{0:T(1024)S(1)}, s32[896]{0:T(1024)}, u32[]{:S(2)}) copy-start(s32[896]{0:T(1024)} %param.9) | copy-start | bytes 10756
  222.1 227.3 %copy-start.3 = (s32[28]{0:T(128)S(1)}, s32[28]{0:T(128)}, u32[]{:S(2)}) copy-start(s32[28]{0:T(128)} %param.11) | copy-start | bytes 340
  222.1 227.9 %copy-start.2 = (s32[28]{0:T(128)S(1)}, s32[28]{0:T(128)}, u32[]{:S(2)}) copy-start(s32[28]{0:T(128)} %param.10) | copy-start | bytes 340
  450.0 103.3 %copy-start.1 = (f32[28]{0:T(128)}, f32[28]{0:T(128)S(1)}, u32[]{:S(2)}) copy-start(f32[28]{0:T(128)S(1)} %get-tuple-element.15) | copy-start | bytes 340
Sparse Core Ops, SparseCore 0:
  11.0 77.1 all-gather.3
  90.3 117.0 all-gather.5
where the time goes:
time: 561 us; the launch traced here: 560 us
  blocking collectives  319 us (57%)
  waiting for transfers between devices  170 us (30%)
  local copies, waits for them, and re-layouts  31.9 us (6%)
  matrix products  14.7 us (3%)
  between operations  14.1 us (3%)
  other arithmetic  9.96 us (2%)
    psum x1, blocking collectives, body(): lax.psum((total * scale, (spread + (top - best) * total) * scale, target_...  119 us
    all_gather x1, waiting for transfers between devices, body(): lax.all_gather(head_weight, 'dp', axis=0, tiled=True)  114 us
    psum x1, blocking collectives, body(): seq_sums, seq_live = lax.psum((seq_sums, seq_live), ('dp', 'tensor'))  103 us
    pmax x1, blocking collectives, body(): best = lax.pmax(top, 'tensor')  73.2 us
    all_gather x1, waiting for transfers between devices, body(): lax.all_gather(hidden, 'tensor', axis=1, tiled=True)  54 us
    gather x1, local copies, waits for them, and re-layouts, body(): jnp.take_along_axis(scores, jnp.clip(local_ids, 0, vocab_dev - 1)[:, None...  31.9 us
    all_gather x1, blocking collectives, body(): lax.all_gather(gain, 'tensor', axis=0, tiled=True)  24.1 us
    dot_general x1, matrix products, body(): jnp.dot(normed, lax.all_gather(head_weight, 'dp', axis=0, tiled=True), pr...  14.7 us
  transfers between devices with their start and end apart: 2, of which 2 were waited for; matrix products, arithmetic and copies ran while one was open for 1% of the time, Pallas kernels for 0%

commit v1 on v0

v1 whole, which is shorter than its diff:
```python
import functools

import jax
import jax.numpy as jnp
from jax import lax
from jax.experimental import pallas as pl
from jax.experimental.pallas import tpu as pltpu
from jax.sharding import PartitionSpec as P


SEQS = 64
EXTRA = 16
VM = pl.BlockSpec(memory_space=pltpu.VMEM)
SM = pl.BlockSpec(memory_space=pltpu.SMEM)
NT = (((1,), (1,)), ((), ()))


def room(mib):
    return pltpu.CompilerParams(vmem_limit_bytes=mib << 20)


def cost(flops, nbytes):
    return pl.CostEstimate(flops=int(flops), transcendentals=0, bytes_accessed=int(nbytes))


def fan_kernel(hid_ref, gain_ref, seq_ref, live_ref, out_ref, block_ref, extra_ref, sems):
    copies, rows, _ = out_ref.shape
    share = seq_ref.shape[1]
    extra_ref[...] = jnp.zeros_like(extra_ref)
    extra_ref[0:1, :] = gain_ref[...].astype(jnp.float32)
    extra_ref[1:2, 0:share] = seq_ref[...].astype(jnp.float32)
    extra_ref[2:3, 0:share] = live_ref[...].astype(jnp.float32)
    block_ref[0 : rows - EXTRA, :] = hid_ref[...]
    block_ref[rows - EXTRA : rows, :] = extra_ref[...].astype(jnp.bfloat16)
    moves = [pltpu.make_async_copy(block_ref, out_ref.at[i], sems.at[i]) for i in range(copies)]
    for move in moves:
        move.start()
    for move in moves:
        move.wait()


def fan(hidden, gain, seq_ids, live, copies):
    tokens, lanes = hidden.shape
    return pl.pallas_call(
        fan_kernel,
        out_shape=jax.ShapeDtypeStruct((copies, tokens + EXTRA, lanes), jnp.bfloat16),
        in_specs=[VM] * 4,
        out_specs=pl.BlockSpec(memory_space=pltpu.HBM),
        scratch_shapes=[
            pltpu.VMEM((tokens + EXTRA, lanes), jnp.bfloat16),
            pltpu.VMEM((EXTRA, lanes), jnp.float32),
            pltpu.SemaphoreType.DMA((copies,)),
        ],
        compiler_params=room(4),
        name="fan",
    )(hidden, gain[None], seq_ids[None], live[None])


def norm_kernel(core_ref, one_ref, two_ref, out_ref):
    chips, rows, lanes = one_ref.shape
    tokens = rows - EXTRA
    step = 128
    core = core_ref[0]

    def block(i, carry):
        at = pl.ds(pl.multiple_of(i * step, step), step)
        square = jnp.zeros((step, lanes), jnp.float32)
        for ref in (one_ref, two_ref):
            for t in range(chips):
                v = ref[t, at, :].astype(jnp.float32)
                square = square + v * v
        mean = jnp.sum(square, axis=-1, keepdims=True) / (2 * chips * lanes)
        scale = lax.rsqrt(mean + 1e-05)
        for ref, half in ((one_ref, core), (two_ref, 1 - core)):
            to = pl.ds(pl.multiple_of(half * lanes, lanes), lanes)
            for t in range(chips):
                v = ref[t, at, :].astype(jnp.float32)
                gain = ref[t, tokens:rows, :].astype(jnp.float32)[0:1, :]
                out_ref[t, at, to] = (v * scale * gain).astype(jnp.bfloat16)
        return carry

    lax.fori_loop(0, tokens // step, block, 0)


def normalise(core, one, two):
    chips, rows, lanes = one.shape
    tokens = rows - EXTRA
    return pl.pallas_call(
        norm_kernel,
        out_shape=jax.ShapeDtypeStruct((chips, tokens, 2 * lanes), jnp.bfloat16),
        in_specs=[SM, VM, VM],
        out_specs=VM,
        compiler_params=room(20),
        cost_estimate=cost(12 * one.size, 8 * one.size),
        name="norm",
    )(core, one, two)


def product(w, x):
    return lax.dot_general(w, x, NT, preferred_element_type=jnp.float32)


def blocks_of(tokens, width=256):
    return [slice(i, min(i + width, tokens)) for i in range(0, tokens, width)]


def mm_kernel(count, fresh, at_ref, n_ref, *refs):
    ws, out_ref = refs[:count], refs[-1]
    for cols in blocks_of(n_ref.shape[1]):
        total = None if fresh else refs[count][:, cols]
        for i in range(count):
            d = product(ws[i][...], n_ref[at_ref[i], cols, :])
            total = d if total is None else total + d
        out_ref[:, cols] = total


def accumulate(at, normed, ws, acc=None):
    vocab, depth = ws[0].shape
    tokens = normed.shape[1]
    return pl.pallas_call(
        functools.partial(mm_kernel, len(ws), acc is None),
        out_shape=jax.ShapeDtypeStruct((vocab, tokens), jnp.float32),
        in_specs=[SM, VM] + [VM] * len(ws) + ([] if acc is None else [VM]),
        out_specs=VM,
        input_output_aliases={} if acc is None else {2 + len(ws): 0},
        compiler_params=room(26),
        cost_estimate=cost(2 * len(ws) * vocab * depth * tokens, 8 * vocab * tokens),
        name="scores",
    )(at, normed, *ws, *([] if acc is None else [acc]))


def stats_kernel(at_ref, n_ref, w_ref, acc_ref, ids_ref, out_ref, s_ref):
    _, tokens = acc_ref.shape
    for cols in blocks_of(tokens):
        s_ref[:, cols] = acc_ref[:, cols] + product(w_ref[...], n_ref[at_ref[0], cols, :])
    for j in range(tokens // 128):
        at = slice(j * 128, (j + 1) * 128)
        s = s_ref[:, at]
        top = jnp.max(s, axis=0, keepdims=True)
        row = lax.broadcasted_iota(jnp.int32, s.shape, 0)
        picked = jnp.sum(jnp.where(row == ids_ref[:, at], s, 0.0), axis=0, keepdims=True)
        shifted = s - top
        expo = jnp.exp(shifted)
        total = jnp.sum(expo, axis=0, keepdims=True)
        spread = jnp.sum(expo * shifted, axis=0, keepdims=True)
        out_ref[0:1, at] = top
        out_ref[1:2, at] = total
        out_ref[2:3, at] = spread
        out_ref[3:4, at] = picked


def statistics(at, normed, w, acc, ids):
    vocab, tokens = acc.shape
    return pl.pallas_call(
        stats_kernel,
        out_shape=jax.ShapeDtypeStruct((4, tokens), jnp.float32),
        in_specs=[SM, VM, VM, VM, VM],
        out_specs=VM,
        scratch_shapes=[pltpu.VMEM((vocab, tokens), jnp.float32)],
        compiler_params=room(26),
        cost_estimate=cost(2 * vocab * w.shape[1] * tokens, 8 * vocab * tokens),
        name="stats",
    )(at, normed, w, acc, ids)


def combine_kernel(x_ref, seq_ref, live_ref, logprob_ref, entropy_ref, sums_ref):
    top = x_ref[:, 0, :]
    total = x_ref[:, 1, :]
    best = jnp.max(top, axis=0, keepdims=True)
    gap = top - best
    scale = jnp.exp(gap)
    g_total = jnp.sum(total * scale, axis=0, keepdims=True)
    g_spread = jnp.sum((x_ref[:, 2, :] + gap * total) * scale, axis=0, keepdims=True)
    g_target = jnp.sum(x_ref[:, 3, :], axis=0, keepdims=True)
    live = live_ref[...]
    log_total = jnp.log(g_total)
    logprob = (g_target - best - log_total) * live
    logprob_ref[...] = logprob
    entropy_ref[...] = (log_total - g_spread / g_total) * live
    tokens = top.shape[1]
    row = lax.broadcasted_iota(jnp.int32, (8, tokens), 0)
    both = jnp.where(row == 0, logprob, jnp.where(row == 1, live, 0.0))
    seat = lax.broadcasted_iota(jnp.int32, (2 * SEQS, tokens), 0) % SEQS
    member = (seat == seq_ref[...]).astype(jnp.float32)
    sums = lax.dot_general(
        both, member, NT, precision=lax.Precision.HIGHEST, preferred_element_type=jnp.float32
    )
    lane = lax.broadcasted_iota(jnp.int32, (1, 2 * SEQS), 1)
    sums_ref[...] = jnp.where(lane < SEQS, sums[0:1, :], sums[1:2, :])


def combine(x, seq, live):
    tokens = x.shape[2]
    row = jax.ShapeDtypeStruct((1, tokens), jnp.float32)
    return pl.pallas_call(
        combine_kernel,
        out_shape=(row, row, jax.ShapeDtypeStruct((1, 2 * SEQS), jnp.float32)),
        in_specs=[VM] * 3,
        out_specs=(VM, VM, VM),
        compiler_params=room(8),
        name="combine",
    )(x, seq, live)


def body(hidden, gain, head_weight, targets, seq_ids, live):
    shards = lax.axis_size("tensor")
    ring = lax.axis_size("dp")
    rank, z = lax.axis_index("tensor"), lax.axis_index("dp")
    tokens = hidden.shape[0]
    share = tokens // shards
    vocab_dev = head_weight.shape[1]

    forth = [(i, (i + 1) % ring) for i in range(ring)]
    back = [(i, (i - 1) % ring) for i in range(ring)]
    own = head_weight.T
    chunks = [own]

    def turn(a, b, s):
        a = lax.ppermute(a, "dp", forth)
        if s < ring - s:
            b = lax.ppermute(b, "dp", back)
            return a, b
        return a, None

    tie = lax.optimization_barrier
    a, b = turn(own, own, 1)
    core = rank % 2
    teams = [[t for t in range(shards) if t % 2 == c] for c in range(2)]
    sent = fan(hidden, gain, seq_ids, live, shards // 2)
    one = lax.all_to_all(sent, "tensor", 0, 0, axis_index_groups=teams)
    chunks += [a, b]
    for s in range(2, 5):
        a, b = turn(a, b, s)
        if s == 4:
            a, b, one = tie((a, b, one))
        chunks += [a, b]
    two = lax.ppermute(one, "tensor", [(t, t ^ 1) for t in range(shards)])
    a, b = turn(a, b, 5)
    chunks += [a, b]
    normed = normalise(core[None].astype(jnp.int32), one, two)

    def pick(lo, hi):
        span = [z] + [z + (s if i else -s) for s in range(1, ring // 2 + 1) for i in range(2)]
        return (jnp.stack(span[lo:hi]) % ring).astype(jnp.int32)

    a, b = turn(a, b, 6)
    a, b, normed = tie((a, b, normed))
    chunks += [a, b]
    acc = accumulate(pick(0, 9), normed, chunks[0:9])
    a, b = turn(a, b, 7)
    a, b, acc = tie((a, b, acc))
    chunks += [a, b]
    acc = accumulate(pick(9, 15), normed, chunks[9:15], acc)
    a, _ = turn(a, b, 8)
    flags = jnp.stack([one, two])[:, :, tokens + 1 : tokens + 3, :share].astype(jnp.float32)
    flags = jnp.where(core == 0, flags, flags[::-1]).transpose(2, 1, 0, 3).reshape(2, 1, tokens)
    seq, alive = flags[0].astype(jnp.int32), flags[1]
    stats = statistics(pick(15, 16), normed, a, acc, (targets - rank * vocab_dev)[None])

    everyone = lax.all_to_all(
        jnp.broadcast_to(stats[None], (shards, *stats.shape)), "tensor", 0, 0
    )
    logprob, entropy, sums = combine(everyone, seq, alive)
    planes = lax.all_to_all(jnp.broadcast_to(sums, (ring, 2 * SEQS)), "dp", 0, 0)
    whole = jnp.sum(planes, axis=0)
    seq_mean = whole[:SEQS] / jnp.maximum(whole[SEQS:], 1.0)
    mine = functools.partial(lax.dynamic_slice_in_dim, start_index=rank * share, slice_size=share)
    return mine(logprob[0]), mine(entropy[0]), seq_mean


def solution(mesh):
    placed = (
        P("dp", "tensor"),
        P("tensor"),
        P("dp", "tensor"),
        P("dp"),
        P(("dp", "tensor")),
        P(("dp", "tensor")),
    )

    return jax.shard_map(
        body,
        mesh=mesh,
        in_specs=placed,
        out_specs=(P(("dp", "tensor")), P(("dp", "tensor")), P()),
        check_vma=False,
    )
```

time: 561 us -> 200 us (0.36)
  blocking collectives: 319 us -> 0 us
  waiting for transfers between devices: 170 us -> 75.5 us
  starting transfers between devices: 0.08 us -> 86.6 us
  Pallas kernels: 0 us -> 25.7 us
  local copies, waits for them, and re-layouts: 31.9 us -> 8.8 us
  matrix products: 14.7 us -> 0 us
  between operations: 14.1 us -> 1.04 us
  other arithmetic: 9.96 us -> 1.47 us
    psum x2 -> x0, blocking collectives: 222 us -> none  [the longest x1 119 us: body(): lax.psum((total * scale, (spread + (top - best) * total) * scale, target_...]
    all_gather x2 -> x0, waiting for transfers between devices: 169 us -> none  [the longest x1 114 us: body(): lax.all_gather(head_weight, 'dp', axis=0, tiled=True)]
    pmax x1 -> x0, blocking collectives: 73.2 us -> none  [body(): best = lax.pmax(top, 'tensor')]
    ppermute x0 -> x16, starting transfers between devices: none -> 63.4 us  [the longest x7 41.8 us: turn(): b = lax.ppermute(b, 'dp', back)]
    ppermute x0 -> x16, waiting for transfers between devices: none -> 54.2 us  [the longest x7 29.1 us: turn(): b = lax.ppermute(b, 'dp', back)]
    gather x1 -> x0, local copies, waits for them, and re-layouts: 31.9 us -> none  [body(): jnp.take_along_axis(scores, jnp.clip(local_ids, 0, vocab_dev - 1)[:, None...]
    pallas_call x0 -> x6, Pallas kernels: none -> 25.7 us  [the longest x2 11 us: accumulate(): pl.pallas_call(functools.partial(mm_kernel, len(ws), acc is None), out_sh...]
    all_gather x1 -> x0, blocking collectives: 24.1 us -> none  [body(): lax.all_gather(gain, 'tensor', axis=0, tiled=True)]
  transfers between devices with their start and end apart: 2 -> 19, of which waited for: 2 -> 13; matrix products, arithmetic and copies ran while one was open for 1% -> 1% of each run, Pallas kernels for 0% -> 9%
where the time goes in v1:
time: 200 us; the launch traced here: 199 us
  starting transfers between devices  86.6 us (43%)
  waiting for transfers between devices  75.5 us (38%)
  Pallas kernels  25.7 us (13%)
  local copies, waits for them, and re-layouts  8.8 us (4%)
    ppermute x7, starting transfers between devices, turn(): b = lax.ppermute(b, 'dp', back)  41.8 us
    ppermute x7, waiting for transfers between devices, turn(): b = lax.ppermute(b, 'dp', back)  29.1 us
    ppermute x8, waiting for transfers between devices, turn(): a = lax.ppermute(a, 'dp', forth)  25.2 us
    ppermute x8, starting transfers between devices, turn(): a = lax.ppermute(a, 'dp', forth)  15.3 us
    pallas_call x2, Pallas kernels, accumulate(): pl.pallas_call(functools.partial(mm_kernel, len(ws), acc is None), out_sh...  11 us
    all_to_all x1, waiting for transfers between devices, body(): lax.all_to_all(jnp.broadcast_to(sums, (ring, 2 * SEQS)), 'dp', 0, 0)  10.7 us
    all_to_all x1, waiting for transfers between devices, body(): lax.all_to_all(jnp.broadcast_to(stats[None], (shards, *stats.shape)), 'te...  10.6 us
    all_to_all x1, starting transfers between devices, body(): lax.all_to_all(jnp.broadcast_to(stats[None], (shards, *stats.shape)), 'te...  9.21 us
  transfers between devices with their start and end apart: 19, of which 13 were waited for; matrix products, arithmetic and copies ran while one was open for 1% of the time, Pallas kernels for 9%

profile of v1, /device:TPU:1, one launch (start us, length us, event | category | flops | bytes accessed | tf_op | source)
XLA Modules:
  0.0 199.1 jit_solution(16440719036599099741)
XLA Ops:
  0.6 0.0 copy-start.6
  0.6 0.9 copy-done.6
  1.6 0.7 copy-done.7
  2.2 0.7 copy-done.8
  2.9 0.7 copy-done.9
  3.5 5.0 %fan.1 = bf16[16,912,128]{2,1,0:T(8,128)(2,1)S(1)} custom-call(bf16[896,128]{1,0:T(8,128)(2,1)S(1)} %copy-done.6, bf16[1,128]{1,0:T(2,128)(2,1)S(1)} %bitcast.34, s32[1,28]{1,0:T(1,128)S(1)} %bitcast.35, s32[1,28]{1,0:T(1,128)S(1)} %bitcast.36), custom_call_target="tpu_custom_call" | custom-call | tf_op jit(solution)/shard_map/fan/pallas_call | solution.py:44
  8.5 0.0 copy-start
  8.5 1.8 copy-done
  10.4 7.7 %all-to-all-start = ((bf16[16,912,128]{2,1,0:T(8,128)(2,1)}), bf16[16,912,128]{2,1,0:T(8,128)(2,1)}, u32[]{:S(2)}, u32[]{:S(2)}) async-start(bf16[16,912,128]{2,1,0:T(8,128)(2,1)} %copy-done), calls=%async_computation | async-start | bytes 7471104 | tf_op jit(solution)/shard_map/all_to_all | solution.py:230
  18.1 0.0 copy-done.1
  18.1 11.1 %collective-permute-start.4 = (bf16[1000,256]{1,0:T(8,128)(2,1)S(1)}, bf16[1000,256]{1,0:T(8,128)(2,1)S(1)}, u32[]{:S(2)}, u32[]{:S(2)}) collective-permute-start(bf16[1000,256]{1,0:T(8,128)(2,1)S(1)} %bitcast.31), channel_id=1, source_target_pairs={{0,480},{32,0},{64,32},{96,64},{128,96},{160,128},{192,160},{224,1... | collective-permute-start | bytes 1536008 | tf_op jit(solution)/shard_map/ppermute | solution.py:221
  29.3 1.9 collective-permute-start
  31.2 8.1 %collective-permute-done.4.refs_2_ = bf16[1000,256]{1,0:T(8,128)(2,1)S(1)} collective-permute-done((bf16[1000,256]{1,0:T(8,128)(2,1)S(1)}, bf16[1000,256]{1,0:T(8,128)(2,1)S(1)}, u32[]{:S(2)}, u32[]{:S(2)}) %collective-permute-start.4) | collective-permute-done | bytes 512032 | tf_op jit(solution)/shard_map/ppermute | solution.py:221
  39.3 5.4 %collective-permute-start.5 = (bf16[1000,256]{1,0:T(8,128)(2,1)S(1)}, bf16[1000,256]{1,0:T(8,128)(2,1)S(1)}, u32[]{:S(2)}, u32[]{:S(2)}) collective-permute-start(bf16[1000,256]{1,0:T(8,128)(2,1)S(1)} %collective-permute-done.4.refs_2_), channel_id=1, source_target_pairs={{0,480},{32,0},{64,32},{96,64},{128,96},{160,128},{192,160},{224,1... | collective-permute-start | bytes 1536008 | tf_op jit(solution)/shard_map/ppermute | solution.py:221
  44.7 0.0 collective-permute-done.refs_1_
  44.7 1.9 collective-permute-start.1
  46.7 7.4 %collective-permute-done.5.refs_4_ = bf16[1000,256]{1,0:T(8,128)(2,1)S(1)} collective-permute-done((bf16[1000,256]{1,0:T(8,128)(2,1)S(1)}, bf16[1000,256]{1,0:T(8,128)(2,1)S(1)}, u32[]{:S(2)}, u32[]{:S(2)}) %collective-permute-start.5) | collective-permute-done | bytes 512032 | tf_op jit(solution)/shard_map/ppermute | solution.py:221
  54.0 5.4 %collective-permute-start.6 = (bf16[1000,256]{1,0:T(8,128)(2,1)S(1)}, bf16[1000,256]{1,0:T(8,128)(2,1)S(1)}, u32[]{:S(2)}, u32[]{:S(2)}) collective-permute-start(bf16[1000,256]{1,0:T(8,128)(2,1)S(1)} %collective-permute-done.5.refs_4_), channel_id=1, source_target_pairs={{0,480},{32,0},{64,32},{96,64},{128,96},{160,128},{192,160},{224,1... | collective-permute-start | bytes 1536008 | tf_op jit(solution)/shard_map/ppermute | solution.py:221
  59.4 0.0 collective-permute-done.1.refs_3_
  59.4 1.9 collective-permute-start.2
  61.4 6.6 %collective-permute-done.6.refs_6_ = bf16[1000,256]{1,0:T(8,128)(2,1)S(1)} collective-permute-done((bf16[1000,256]{1,0:T(8,128)(2,1)S(1)}, bf16[1000,256]{1,0:T(8,128)(2,1)S(1)}, u32[]{:S(2)}, u32[]{:S(2)}) %collective-permute-start.6) | collective-permute-done | bytes 512032 | tf_op jit(solution)/shard_map/ppermute | solution.py:221
  68.0 5.4 %collective-permute-start.7 = (bf16[1000,256]{1,0:T(8,128)(2,1)S(1)}, bf16[1000,256]{1,0:T(8,128)(2,1)S(1)}, u32[]{:S(2)}, u32[]{:S(2)}) collective-permute-start(bf16[1000,256]{1,0:T(8,128)(2,1)S(1)} %collective-permute-done.6.refs_6_), channel_id=1, source_target_pairs={{0,480},{32,0},{64,32},{96,64},{128,96},{160,128},{192,160},{224,1... | collective-permute-start | bytes 1536008 | tf_op jit(solution)/shard_map/ppermute | solution.py:221
  73.4 0.0 collective-permute-done.2.refs_5_
  73.4 1.9 collective-permute-start.3
  75.3 0.0 copy-start.2
  75.3 0.8 copy-done.2
  76.1 5.1 %collective-permute-done.7.refs_8_ = bf16[1000,256]{1,0:T(8,128)(2,1)S(1)} collective-permute-done((bf16[1000,256]{1,0:T(8,128)(2,1)S(1)}, bf16[1000,256]{1,0:T(8,128)(2,1)S(1)}, u32[]{:S(2)}, u32[]{:S(2)}) %collective-permute-start.7) | collective-permute-done | bytes 512032 | tf_op jit(solution)/shard_map/ppermute | solution.py:221
  81.2 0.8 copy-done.4
  82.0 4.3 %collective-permute-done.3.refs_7_ = bf16[1000,256]{1,0:T(8,128)(2,1)} collective-permute-done((bf16[1000,256]{1,0:T(8,128)(2,1)S(1)}, bf16[1000,256]{1,0:T(8,128)(2,1)}, u32[]{:S(2)}, u32[]{:S(2)}) %collective-permute-start.3) | collective-permute-done | bytes 512032 | tf_op jit(solution)/shard_map/ppermute | solution.py:219
  86.3 0.0 all-to-all-done.one_ref
  86.3 6.2 %collective-permute-start.12 = (bf16[16,912,128]{2,1,0:T(8,128)(2,1)}, bf16[16,912,128]{2,1,0:T(8,128)(2,1)}, u32[]{:S(2)}, u32[]{:S(2)}) collective-permute-start(bf16[16,912,128]{2,1,0:T(8,128)(2,1)} %all-to-all-done.one_ref), channel_id=1, source_target_pairs={{0,1},{1,0},{2,3},{3,2},{4,5},{5,4},{6,7},{7,6},{8,9},{9,8},{10,11... | collective-permute-start | bytes 11206664 | tf_op jit(solution)/shard_map/ppermute | solution.py:237
  92.6 1.9 collective-permute-start.8
  94.5 4.6 %collective-permute-start.10 = (bf16[1000,256]{1,0:T(8,128)(2,1)}, bf16[1000,256]{1,0:T(8,128)(2,1)}, u32[]{:S(2)}, u32[]{:S(2)}) collective-permute-start(bf16[1000,256]{1,0:T(8,128)(2,1)} %copy-done.4), channel_id=1, source_target_pairs={{0,480},{32,0},{64,32},{96,64},{128,96},{160,128},{192,160},{224,1... | collective-permute-start | bytes 1536008 | tf_op jit(solution)/shard_map/ppermute | solution.py:221
  99.1 10.1 %collective-permute-done.8.refs_0_ = bf16[1000,256]{1,0:T(8,128)(2,1)} collective-permute-done((bf16[1000,256]{1,0:T(8,128)(2,1)}, bf16[1000,256]{1,0:T(8,128)(2,1)}, u32[]{:S(2)}, u32[]{:S(2)}) %collective-permute-start.8) | collective-permute-done | bytes 512032 | tf_op jit(solution)/shard_map/ppermute | solution.py:219
  109.2 1.9 collective-permute-start.9
  111.1 0.0 collective-permute-done.10.refs_1_
  111.2 4.6 %collective-permute-start.11 = (bf16[1000,256]{1,0:T(8,128)(2,1)}, bf16[1000,256]{1,0:T(8,128)(2,1)}, u32[]{:S(2)}, u32[]{:S(2)}) collective-permute-start(bf16[1000,256]{1,0:T(8,128)(2,1)} %collective-permute-done.10.refs_1_), channel_id=1, source_target_pairs={{0,480},{32,0},{64,32},{96,64},{128,96},{160,128},{192,160},{224,1... | collective-permute-start | bytes 1536008 | tf_op jit(solution)/shard_map/ppermute | solution.py:221
  115.8 0.1 stack.80
  115.9 0.1 stack.73
  116.0 0.0 collective-permute-done.12.two_ref
  116.0 7.2 %norm.1.n_ref = bf16[16,896,256]{2,1,0:T(8,128)(2,1)S(1)} custom-call(s32[1]{0:T(128)} %bitcast.5.core_ref, bf16[16,912,128]{2,1,0:T(8,128)(2,1)} %all-to-all-done.one_ref, bf16[16,912,128]{2,1,0:T(8,128)(2,1)} %collective-permute-done.12.two_ref), custom_call_target="tpu_custom_call" | custom-call | flops 22413312 | bytes 14942208 | tf_op jit(solution)/shard_map/norm/pallas_call | solution.py:88
  123.2 1.8 collective-permute-done.9.refs_2_
  125.0 0.9 collective-permute-done.11.refs_3_
  125.9 1.9 collective-permute-start.13
  127.8 5.3 %collective-permute-start.14 = (bf16[1000,256]{1,0:T(8,128)(2,1)}, bf16[1000,256]{1,0:T(8,128)(2,1)S(1)}, u32[]{:S(2)}, u32[]{:S(2)}) collective-permute-start(bf16[1000,256]{1,0:T(8,128)(2,1)} %collective-permute-done.11.refs_3_), channel_id=1, source_target_pairs={{0,480},{32,0},{64,32},{96,64},{128,96},{160,128},{192,160},{224,1... | collective-permute-start | bytes 1536008 | tf_op jit(solution)/shard_map/ppermute | solution.py:221
  133.2 6.0 %scores.2.refs_6_ = f32[1000,896]{1,0:T(8,128)S(1)} custom-call(s32[9]{0:T(128)S(1)} %and_select_fusion.1.at_ref, bf16[16,896,256]{2,1,0:T(8,128)(2,1)S(1)} %norm.1.n_ref, bf16[1000,256]{1,0:T(8,128)(2,1)S(1)} %bitcast.33, bf16[1000,256]{1,0:T(8,128)(2,1)S(1)} %collective-permute-done.refs_1_, bf16[1000,256]{1,0:T(8,128)(2,1)S(1)} %collective-permute-done.4.refs_2_, ...), custom_call_target="tpu_custom_call" | custom-call | flops 4128768000 | bytes 7168000 | tf_op jit(solution)/shard_map/scores/pallas_call | solution.py:120
  139.2 2.2 %collective-permute-done.13.refs_4_ = bf16[1000,256]{1,0:T(8,128)(2,1)S(1)} collective-permute-done((bf16[1000,256]{1,0:T(8,128)(2,1)}, bf16[1000,256]{1,0:T(8,128)(2,1)S(1)}, u32[]{:S(2)}, u32[]{:S(2)}) %collective-permute-start.13) | collective-permute-done | bytes 512032 | tf_op jit(solution)/shard_map/ppermute | solution.py:219
  141.4 1.0 collective-permute-done.14.refs_5_
  142.4 1.9 collective-permute-start.15
  144.4 0.8 fusion.1
  145.2 4.9 %scores.3.acc_ref = f32[1000,896]{1,0:T(8,128)S(1)} custom-call(s32[6]{0:T(128)S(1)} %and_select_fusion.at_ref, bf16[16,896,256]{2,1,0:T(8,128)(2,1)S(1)} %norm.1.n_ref, bf16[1000,256]{1,0:T(8,128)(2,1)} %collective-permute-done.8.refs_0_, bf16[1000,256]{1,0:T(8,128)(2,1)} %collective-permute-done.10.refs_1_, ...), custom_call_target="tpu_custom_call", output_to_operand_aliasing={{}: (8, {})} | custom-call | flops 2752512000 | bytes 7168000 | tf_op jit(solution)/shard_map/scores/pallas_call | solution.py:120
  150.1 6.7 %collective-permute-done.15.w_ref = bf16[1000,256]{1,0:T(8,128)(2,1)S(1)} collective-permute-done((bf16[1000,256]{1,0:T(8,128)(2,1)S(1)}, bf16[1000,256]{1,0:T(8,128)(2,1)S(1)}, u32[]{:S(2)}, u32[]{:S(2)}) %collective-permute-start.15) | collective-permute-done | bytes 512032 | tf_op jit(solution)/shard_map/ppermute | solution.py:219
  156.8 1.9 stats.1
  158.7 0.8 broadcast_in_dim.31
  159.5 9.2 %all-to-all-start.1 = ((f32[32,4,896]{2,1,0:T(4,128)}), f32[32,4,896]{2,1,0:T(4,128)S(1)}, u32[]{:S(2)}, u32[]{:S(2)}) async-start(f32[32,4,896]{2,1,0:T(4,128)} %broadcast_in_dim.31), calls=%async_computation.1 | async-start | bytes 917504 | tf_op jit(solution)/shard_map/all_to_all | solution.py:260
  168.8 0.1 squeeze.2.live_ref
  169.0 0.1 convert_element_type.10.seq_ref
  169.1 10.6 %all-to-all-done.1.x_ref = f32[32,4,896]{2,1,0:T(4,128)S(1)} async-done(((f32[32,4,896]{2,1,0:T(4,128)}), f32[32,4,896]{2,1,0:T(4,128)S(1)}, u32[]{:S(2)}, u32[]{:S(2)}) %all-to-all-start.1) | async-done | bytes 458784 | tf_op jit(solution)/shard_map/all_to_all | solution.py:260
  179.7 0.7 combine.1
  180.4 0.6 broadcast_in_dim.32
  181.0 6.3 %all-to-all-start.2 = ((f32[16,1,128]{2,1,0:T(1,128)}), f32[16,1,128]{2,1,0:T(1,128)S(1)}, u32[]{:S(2)}, u32[]{:S(2)}) async-start(f32[16,1,128]{2,1,0:T(1,128)} %broadcast_in_dim.32), calls=%async_computation.2 | async-start | bytes 16384 | tf_op jit(solution)/shard_map/all_to_all | solution.py:264
  187.3 0.6 dynamic-slice_bitcast_fusion
  187.9 10.7 %all-to-all-done.2 = f32[16,1,128]{2,1,0:T(1,128)S(1)} async-done(((f32[16,1,128]{2,1,0:T(1,128)}), f32[16,1,128]{2,1,0:T(1,128)S(1)}, u32[]{:S(2)}, u32[]{:S(2)}) %all-to-all-start.2) | async-done | bytes 8224 | tf_op jit(solution)/shard_map/all_to_all | solution.py:264
  198.5 0.6 maximum_divide_fusion
  (20 shorter events, 0.1 us)
Async XLA Ops:
  0.6 0.9 copy-start.6
  1.6 0.7 copy-start.7
  2.2 0.7 copy-start.8
  2.9 0.7 copy-start.9
  8.5 1.8 copy-start
  10.4 7.8 %copy-start.1 = (bf16[256,1000]{0,1:T(8,128)(2,1)S(1)}, bf16[256,1000]{0,1:T(8,128)(2,1)}, u32[]{:S(2)}) copy-start(bf16[256,1000]{0,1:T(8,128)(2,1)} %param.8) | copy-start | bytes 1536004
  10.4 105.4 %copy-start.10 = (s32[896]{0:T(1024)S(1)}, s32[896]{0:T(1024)}, u32[]{:S(2)}) copy-start(s32[896]{0:T(1024)} %param.9) | copy-start | bytes 10756
  10.4 76.0 %all-to-all-start = ((bf16[16,912,128]{2,1,0:T(8,128)(2,1)}), bf16[16,912,128]{2,1,0:T(8,128)(2,1)}, u32[]{:S(2)}, u32[]{:S(2)}) async-start(bf16[16,912,128]{2,1,0:T(8,128)(2,1)} %copy-done), calls=%async_computation | async-start | bytes 7471104 | tf_op jit(solution)/shard_map/all_to_all | solution.py:230
  18.1 21.2 %collective-permute-start.4 = (bf16[1000,256]{1,0:T(8,128)(2,1)S(1)}, bf16[1000,256]{1,0:T(8,128)(2,1)S(1)}, u32[]{:S(2)}, u32[]{:S(2)}) collective-permute-start(bf16[1000,256]{1,0:T(8,128)(2,1)S(1)} %bitcast.31), channel_id=1, source_target_pairs={{0,480},{32,0},{64,32},{96,64},{128,96},{160,128},{192,160},{224,1... | collective-permute-start | bytes 1536008 | tf_op jit(solution)/shard_map/ppermute | solution.py:221
  29.3 15.5 %collective-permute-start = (bf16[1000,256]{1,0:T(8,128)(2,1)S(1)}, bf16[1000,256]{1,0:T(8,128)(2,1)S(1)}, u32[]{:S(2)}, u32[]{:S(2)}) collective-permute-start(bf16[1000,256]{1,0:T(8,128)(2,1)S(1)} %bitcast.32), channel_id=1, source_target_pairs={{0,32},{32,64},{64,96},{96,128},{128,160},{160,192},{192,224},{224... | collective-permute-start | bytes 1536008 | tf_op jit(solution)/shard_map/ppermute | solution.py:219
  39.3 14.7 %collective-permute-start.5 = (bf16[1000,256]{1,0:T(8,128)(2,1)S(1)}, bf16[1000,256]{1,0:T(8,128)(2,1)S(1)}, u32[]{:S(2)}, u32[]{:S(2)}) collective-permute-start(bf16[1000,256]{1,0:T(8,128)(2,1)S(1)} %collective-permute-done.4.refs_2_), channel_id=1, source_target_pairs={{0,480},{32,0},{64,32},{96,64},{128,96},{160,128},{192,160},{224,1... | collective-permute-start | bytes 1536008 | tf_op jit(solution)/shard_map/ppermute | solution.py:221
  44.7 14.7 %collective-permute-start.1 = (bf16[1000,256]{1,0:T(8,128)(2,1)S(1)}, bf16[1000,256]{1,0:T(8,128)(2,1)S(1)}, u32[]{:S(2)}, u32[]{:S(2)}) collective-permute-start(bf16[1000,256]{1,0:T(8,128)(2,1)S(1)} %collective-permute-done.refs_1_), channel_id=1, source_target_pairs={{0,32},{32,64},{64,96},{96,128},{128,160},{160,192},{192,224},{224... | collective-permute-start | bytes 1536008 | tf_op jit(solution)/shard_map/ppermute | solution.py:219
  54.0 14.0 %collective-permute-start.6 = (bf16[1000,256]{1,0:T(8,128)(2,1)S(1)}, bf16[1000,256]{1,0:T(8,128)(2,1)S(1)}, u32[]{:S(2)}, u32[]{:S(2)}) collective-permute-start(bf16[1000,256]{1,0:T(8,128)(2,1)S(1)} %collective-permute-done.5.refs_4_), channel_id=1, source_target_pairs={{0,480},{32,0},{64,32},{96,64},{128,96},{160,128},{192,160},{224,1... | collective-permute-start | bytes 1536008 | tf_op jit(solution)/shard_map/ppermute | solution.py:221
  59.4 14.0 %collective-permute-start.2 = (bf16[1000,256]{1,0:T(8,128)(2,1)S(1)}, bf16[1000,256]{1,0:T(8,128)(2,1)S(1)}, u32[]{:S(2)}, u32[]{:S(2)}) collective-permute-start(bf16[1000,256]{1,0:T(8,128)(2,1)S(1)} %collective-permute-done.1.refs_3_), channel_id=1, source_target_pairs={{0,32},{32,64},{64,96},{96,128},{128,160},{160,192},{192,224},{224... | collective-permute-start | bytes 1536008 | tf_op jit(solution)/shard_map/ppermute | solution.py:219
  68.0 13.2 %collective-permute-start.7 = (bf16[1000,256]{1,0:T(8,128)(2,1)S(1)}, bf16[1000,256]{1,0:T(8,128)(2,1)S(1)}, u32[]{:S(2)}, u32[]{:S(2)}) collective-permute-start(bf16[1000,256]{1,0:T(8,128)(2,1)S(1)} %collective-permute-done.6.refs_6_), channel_id=1, source_target_pairs={{0,480},{32,0},{64,32},{96,64},{128,96},{160,128},{192,160},{224,1... | collective-permute-start | bytes 1536008 | tf_op jit(solution)/shard_map/ppermute | solution.py:221
  73.4 12.9 %collective-permute-start.3 = (bf16[1000,256]{1,0:T(8,128)(2,1)S(1)}, bf16[1000,256]{1,0:T(8,128)(2,1)}, u32[]{:S(2)}, u32[]{:S(2)}) collective-permute-start(bf16[1000,256]{1,0:T(8,128)(2,1)S(1)} %collective-permute-done.2.refs_5_), channel_id=1, source_target_pairs={{0,32},{32,64},{64,96},{96,128},{128,160},{160,192},{192,224},{224... | collective-permute-start | bytes 1536008 | tf_op jit(solution)/shard_map/ppermute | solution.py:219
  75.3 0.8 copy-start.2
  81.2 0.8 copy-start.4
  86.3 29.6 %collective-permute-start.12 = (bf16[16,912,128]{2,1,0:T(8,128)(2,1)}, bf16[16,912,128]{2,1,0:T(8,128)(2,1)}, u32[]{:S(2)}, u32[]{:S(2)}) collective-permute-start(bf16[16,912,128]{2,1,0:T(8,128)(2,1)} %all-to-all-done.one_ref), channel_id=1, source_target_pairs={{0,1},{1,0},{2,3},{3,2},{4,5},{5,4},{6,7},{7,6},{8,9},{9,8},{10,11... | collective-permute-start | bytes 11206664 | tf_op jit(solution)/shard_map/ppermute | solution.py:237
  92.6 16.6 %collective-permute-start.8 = (bf16[1000,256]{1,0:T(8,128)(2,1)}, bf16[1000,256]{1,0:T(8,128)(2,1)}, u32[]{:S(2)}, u32[]{:S(2)}) collective-permute-start(bf16[1000,256]{1,0:T(8,128)(2,1)} %collective-permute-done.3.refs_7_), channel_id=1, source_target_pairs={{0,32},{32,64},{64,96},{96,128},{128,160},{160,192},{192,224},{224... | collective-permute-start | bytes 1536008 | tf_op jit(solution)/shard_map/ppermute | solution.py:219
  94.5 16.6 %collective-permute-start.10 = (bf16[1000,256]{1,0:T(8,128)(2,1)}, bf16[1000,256]{1,0:T(8,128)(2,1)}, u32[]{:S(2)}, u32[]{:S(2)}) collective-permute-start(bf16[1000,256]{1,0:T(8,128)(2,1)} %copy-done.4), channel_id=1, source_target_pairs={{0,480},{32,0},{64,32},{96,64},{128,96},{160,128},{192,160},{224,1... | collective-permute-start | bytes 1536008 | tf_op jit(solution)/shard_map/ppermute | solution.py:221
  109.2 15.8 %collective-permute-start.9 = (bf16[1000,256]{1,0:T(8,128)(2,1)}, bf16[1000,256]{1,0:T(8,128)(2,1)}, u32[]{:S(2)}, u32[]{:S(2)}) collective-permute-start(bf16[1000,256]{1,0:T(8,128)(2,1)} %collective-permute-done.8.refs_0_), channel_id=1, source_target_pairs={{0,32},{32,64},{64,96},{96,128},{128,160},{160,192},{192,224},{224... | collective-permute-start | bytes 1536008 | tf_op jit(solution)/shard_map/ppermute | solution.py:219
  111.2 14.7 %collective-permute-start.11 = (bf16[1000,256]{1,0:T(8,128)(2,1)}, bf16[1000,256]{1,0:T(8,128)(2,1)}, u32[]{:S(2)}, u32[]{:S(2)}) collective-permute-start(bf16[1000,256]{1,0:T(8,128)(2,1)} %collective-permute-done.10.refs_1_), channel_id=1, source_target_pairs={{0,480},{32,0},{64,32},{96,64},{128,96},{160,128},{192,160},{224,1... | collective-permute-start | bytes 1536008 | tf_op jit(solution)/shard_map/ppermute | solution.py:221
  116.0 17.2 %copy-start.3 = (bf16[1000,256]{1,0:T(8,128)(2,1)S(1)}, bf16[1000,256]{1,0:T(8,128)(2,1)}, u32[]{:S(2)}) copy-start(bf16[1000,256]{1,0:T(8,128)(2,1)} %copy-done.2) | copy-start | bytes 1536004
  116.0 17.2 %copy-start.5 = (bf16[1000,256]{1,0:T(8,128)(2,1)S(1)}, bf16[1000,256]{1,0:T(8,128)(2,1)}, u32[]{:S(2)}) copy-start(bf16[1000,256]{1,0:T(8,128)(2,1)} %copy-done.4) | copy-start | bytes 1536004
  125.9 15.5 %collective-permute-start.13 = (bf16[1000,256]{1,0:T(8,128)(2,1)}, bf16[1000,256]{1,0:T(8,128)(2,1)S(1)}, u32[]{:S(2)}, u32[]{:S(2)}) collective-permute-start(bf16[1000,256]{1,0:T(8,128)(2,1)} %collective-permute-done.9.refs_2_), channel_id=1, source_target_pairs={{0,32},{32,64},{64,96},{96,128},{128,160},{160,192},{192,224},{224... | collective-permute-start | bytes 1536008 | tf_op jit(solution)/shard_map/ppermute | solution.py:219
  127.8 14.6 %collective-permute-start.14 = (bf16[1000,256]{1,0:T(8,128)(2,1)}, bf16[1000,256]{1,0:T(8,128)(2,1)S(1)}, u32[]{:S(2)}, u32[]{:S(2)}) collective-permute-start(bf16[1000,256]{1,0:T(8,128)(2,1)} %collective-permute-done.11.refs_3_), channel_id=1, source_target_pairs={{0,480},{32,0},{64,32},{96,64},{128,96},{160,128},{192,160},{224,1... | collective-permute-start | bytes 1536008 | tf_op jit(solution)/shard_map/ppermute | solution.py:221
  142.4 14.4 %collective-permute-start.15 = (bf16[1000,256]{1,0:T(8,128)(2,1)S(1)}, bf16[1000,256]{1,0:T(8,128)(2,1)S(1)}, u32[]{:S(2)}, u32[]{:S(2)}) collective-permute-start(bf16[1000,256]{1,0:T(8,128)(2,1)S(1)} %collective-permute-done.13.refs_4_), channel_id=1, source_target_pairs={{0,32},{32,64},{64,96},{96,128},{128,160},{160,192},{192,224},{224... | collective-permute-start | bytes 1536008 | tf_op jit(solution)/shard_map/ppermute | solution.py:219
  159.5 20.2 %all-to-all-start.1 = ((f32[32,4,896]{2,1,0:T(4,128)}), f32[32,4,896]{2,1,0:T(4,128)S(1)}, u32[]{:S(2)}, u32[]{:S(2)}) async-start(f32[32,4,896]{2,1,0:T(4,128)} %broadcast_in_dim.31), calls=%async_computation.1 | async-start | bytes 917504 | tf_op jit(solution)/shard_map/all_to_all | solution.py:260
  181.0 17.5 %all-to-all-start.2 = ((f32[16,1,128]{2,1,0:T(1,128)}), f32[16,1,128]{2,1,0:T(1,128)S(1)}, u32[]{:S(2)}, u32[]{:S(2)}) async-start(f32[16,1,128]{2,1,0:T(1,128)} %broadcast_in_dim.32), calls=%async_computation.2 | async-start | bytes 16384 | tf_op jit(solution)/shard_map/all_to_all | solution.py:264

commit v2 on v1

v2 whole, which is shorter than its diff:
```python
import functools

import jax
import jax.numpy as jnp
from jax import lax
from jax.experimental import pallas as pl
from jax.experimental.pallas import tpu as pltpu
from jax.sharding import PartitionSpec as P


SEQS = 64
EXTRA = 16
VM = pl.BlockSpec(memory_space=pltpu.VMEM)
NT = (((1,), (1,)), ((), ()))


def room(mib):
    return pltpu.CompilerParams(vmem_limit_bytes=mib << 20)


def cost(flops, nbytes):
    return pl.CostEstimate(flops=int(flops), transcendentals=0, bytes_accessed=int(nbytes))


def fan_kernel(hid_ref, gain_ref, seq_ref, live_ref, out_ref, block_ref, g_ref, s_ref, l_ref, extra_ref, sems):
    copies, rows, _ = out_ref.shape
    share = seq_ref.shape[1]
    loads = [
        pltpu.make_async_copy(gain_ref, g_ref, sems.at[0]),
        pltpu.make_async_copy(seq_ref, s_ref, sems.at[1]),
        pltpu.make_async_copy(live_ref, l_ref, sems.at[2]),
        pltpu.make_async_copy(hid_ref, block_ref.at[pl.ds(0, rows - EXTRA)], sems.at[3]),
    ]
    for load in loads:
        load.start()
    for load in loads:
        load.wait()
    extra_ref[...] = jnp.zeros_like(extra_ref)
    extra_ref[0:1, :] = g_ref[...].astype(jnp.float32)
    extra_ref[1:2, 0:share] = s_ref[...].astype(jnp.float32)
    extra_ref[2:3, 0:share] = l_ref[...].astype(jnp.float32)
    block_ref[rows - EXTRA : rows, :] = extra_ref[...].astype(jnp.bfloat16)
    moves = [pltpu.make_async_copy(block_ref, out_ref.at[i], sems.at[i]) for i in range(copies)]
    for move in moves:
        move.start()
    for move in moves:
        move.wait()


def fan(hidden, gain, seq_ids, live, copies):
    tokens, lanes = hidden.shape
    share = seq_ids.shape[0]
    return pl.pallas_call(
        fan_kernel,
        out_shape=pltpu.HBM((copies, tokens + EXTRA, lanes), jnp.bfloat16),
        in_specs=[pl.BlockSpec(memory_space=pltpu.HBM)] * 4,
        out_specs=pl.BlockSpec(memory_space=pltpu.HBM),
        scratch_shapes=[
            pltpu.VMEM((tokens + EXTRA, lanes), jnp.bfloat16),
            pltpu.VMEM((1, lanes), jnp.bfloat16),
            pltpu.VMEM((1, share), jnp.int32),
            pltpu.VMEM((1, share), jnp.int32),
            pltpu.VMEM((EXTRA, lanes), jnp.float32),
            pltpu.SemaphoreType.DMA((copies,)),
        ],
        compiler_params=room(4),
        name="fan",
    )(hidden, gain[None], seq_ids[None], live[None])


def norm_kernel(one_ref, two_ref, gain_one_ref, gain_two_ref, out_ref, flag_ref):
    chips, step, lanes = one_ref.shape
    core = lax.axis_index("tensor") % 2

    @pl.when(pl.program_id(0) == 0)
    def _():
        flag_ref[core] = gain_one_ref[...].astype(jnp.float32)
        flag_ref[1 - core] = gain_two_ref[...].astype(jnp.float32)

    square = jnp.zeros((step, lanes), jnp.float32)
    for ref in (one_ref, two_ref):
        for t in range(chips):
            v = ref[t].astype(jnp.float32)
            square = square + v * v
    mean = jnp.sum(square, axis=-1, keepdims=True) / (2 * chips * lanes)
    scale = lax.rsqrt(mean + 1e-05)
    for ref, gain_ref, half in ((one_ref, gain_one_ref, core), (two_ref, gain_two_ref, 1 - core)):
        to = pl.ds(pl.multiple_of(half * lanes, lanes), lanes)
        for t in range(chips):
            gain = gain_ref[t].astype(jnp.float32)[0:1, :]
            out_ref[t, :, to] = (ref[t].astype(jnp.float32) * scale * gain).astype(jnp.bfloat16)


def normalise(one, two):
    chips, rows, lanes = one.shape
    tokens, step = rows - EXTRA, 128
    part = pl.BlockSpec((chips, step, lanes), lambda i: (0, i, 0))
    gain = pl.BlockSpec((chips, EXTRA, lanes), lambda i: (0, tokens // EXTRA, 0))
    return pl.pallas_call(
        norm_kernel,
        grid=(tokens // step,),
        out_shape=(
            jax.ShapeDtypeStruct((chips, tokens, 2 * lanes), jnp.bfloat16),
            jax.ShapeDtypeStruct((2, chips, EXTRA, lanes), jnp.float32),
        ),
        in_specs=[part, part, gain, gain],
        out_specs=(
            pl.BlockSpec((chips, step, 2 * lanes), lambda i: (0, i, 0)),
            pl.BlockSpec((2, chips, EXTRA, lanes), lambda i: (0, 0, 0, 0)),
        ),
        compiler_params=room(8),
        cost_estimate=cost(12 * one.size, 8 * one.size),
        name="norm",
    )(one, two, one, two)


def product(w, x):
    return lax.dot_general(w, x, NT, preferred_element_type=jnp.float32)


def blocks_of(tokens, width=256):
    return [slice(i, min(i + width, tokens)) for i in range(0, tokens, width)]


def row_block(ahead):
    return (lax.axis_index("dp") + ahead) % lax.axis_size("dp")


def mm_kernel(aheads, n_ref, *refs):
    count = len(aheads)
    ws, out_ref = refs[:count], refs[-1]
    fresh = len(refs) == count + 1
    at = [row_block(ahead + n_ref.shape[0]) for ahead in aheads]
    for cols in blocks_of(n_ref.shape[1]):
        total = None if fresh else refs[count][:, cols]
        for i in range(count):
            d = product(ws[i][...], n_ref[at[i], cols, :])
            total = d if total is None else total + d
        out_ref[:, cols] = total


def accumulate(aheads, normed, ws, acc=None):
    vocab, depth = ws[0].shape
    tokens = normed.shape[1]
    return pl.pallas_call(
        functools.partial(mm_kernel, tuple(aheads)),
        out_shape=jax.ShapeDtypeStruct((vocab, tokens), jnp.float32),
        in_specs=[VM] * (1 + len(ws)) + ([] if acc is None else [VM]),
        out_specs=VM,
        input_output_aliases={} if acc is None else {1 + len(ws): 0},
        compiler_params=room(12),
        cost_estimate=cost(2 * len(ws) * vocab * depth * tokens, 8 * vocab * tokens),
        name="scores",
    )(normed, *ws, *([] if acc is None else [acc]))


def stats_kernel(ahead, n_ref, w_ref, acc_ref, ids_ref, out_ref, s_ref):
    vocab, tokens = acc_ref.shape
    at = row_block(ahead)
    first = lax.axis_index("tensor") * vocab
    for cols in blocks_of(tokens):
        s_ref[:, cols] = acc_ref[:, cols] + product(w_ref[...], n_ref[at, cols, :])
    for j in range(tokens // 128):
        at = slice(j * 128, (j + 1) * 128)
        s = s_ref[:, at]
        top = jnp.max(s, axis=0, keepdims=True)
        row = lax.broadcasted_iota(jnp.int32, s.shape, 0)
        picked = jnp.sum(jnp.where(row == ids_ref[at][None] - first, s, 0.0), axis=0, keepdims=True)
        shifted = s - top
        expo = jnp.exp(shifted)
        total = jnp.sum(expo, axis=0, keepdims=True)
        spread = jnp.sum(expo * shifted, axis=0, keepdims=True)
        out_ref[0:1, at] = top
        out_ref[1:2, at] = total
        out_ref[2:3, at] = spread
        out_ref[3:4, at] = picked


def statistics(ahead, normed, w, acc, ids):
    vocab, tokens = acc.shape
    return pl.pallas_call(
        functools.partial(stats_kernel, ahead),
        out_shape=jax.ShapeDtypeStruct((4, tokens), jnp.float32),
        in_specs=[VM] * 4,
        out_specs=VM,
        scratch_shapes=[pltpu.VMEM((vocab, tokens), jnp.float32)],
        compiler_params=room(12),
        cost_estimate=cost(2 * vocab * w.shape[1] * tokens, 8 * vocab * tokens),
        name="stats",
    )(normed, w, acc, ids)


def combine_kernel(x_ref, seq_ref, live_ref, logprob_ref, entropy_ref, sums_ref):
    top = x_ref[:, 0, :]
    total = x_ref[:, 1, :]
    best = jnp.max(top, axis=0, keepdims=True)
    gap = top - best
    scale = jnp.exp(gap)
    g_total = jnp.sum(total * scale, axis=0, keepdims=True)
    g_spread = jnp.sum((x_ref[:, 2, :] + gap * total) * scale, axis=0, keepdims=True)
    g_target = jnp.sum(x_ref[:, 3, :], axis=0, keepdims=True)
    live = live_ref[...]
    log_total = jnp.log(g_total)
    logprob = (g_target - best - log_total) * live
    entropy = (log_total - g_spread / g_total) * live
    tokens = top.shape[1]
    share = logprob_ref.shape[1]
    row = lax.broadcasted_iota(jnp.int32, (8, tokens), 0)
    rows = jnp.where(row == 0, logprob, jnp.where(row == 1, live, jnp.where(row == 2, entropy, 0.0)))
    seat = lax.broadcasted_iota(jnp.int32, (2 * SEQS, tokens), 0)
    member = (seat % SEQS == seq_ref[...]).astype(jnp.float32)
    token = lax.broadcasted_iota(jnp.int32, (2 * SEQS, tokens), 1)
    mine = (token == seat + lax.axis_index("tensor") * share).astype(jnp.float32)
    exact = functools.partial(
        lax.dot_general,
        dimension_numbers=NT,
        precision=lax.Precision.HIGHEST,
        preferred_element_type=jnp.float32,
    )
    sums, own = exact(rows, member), exact(rows, mine)
    lane = lax.broadcasted_iota(jnp.int32, (1, 2 * SEQS), 1)
    sums_ref[...] = jnp.where(lane < SEQS, sums[0:1, :], sums[1:2, :])
    logprob_ref[...] = own[0:1, 0:share]
    entropy_ref[...] = own[2:3, 0:share]


def combine(x, seq, live):
    row = jax.ShapeDtypeStruct((1, x.shape[2] // x.shape[0]), jnp.float32)
    return pl.pallas_call(
        combine_kernel,
        out_shape=(row, row, jax.ShapeDtypeStruct((1, 2 * SEQS), jnp.float32)),
        in_specs=[VM] * 3,
        out_specs=(VM, VM, VM),
        compiler_params=room(8),
        name="combine",
    )(x, seq, live)


def body(hidden, gain, head_weight, targets, seq_ids, live):
    shards = lax.axis_size("tensor")
    ring = lax.axis_size("dp")
    tokens = hidden.shape[0]
    share = tokens // shards

    forth = [(i, (i + 1) % ring) for i in range(ring)]
    back = [(i, (i - 1) % ring) for i in range(ring)]
    own = head_weight.T
    chunks = [own]

    def turn(a, b, s):
        a = lax.ppermute(a, "dp", forth)
        if s < ring - s:
            b = lax.ppermute(b, "dp", back)
            return a, b
        return a, None

    a, b = turn(own, own, 1)
    chunks += [a, b]
    teams = [[t for t in range(shards) if t % 2 == c] for c in range(2)]
    sent = fan(hidden, gain, seq_ids, live, shards // 2)
    one = lax.all_to_all(sent, "tensor", 0, 0, axis_index_groups=teams)
    two = lax.ppermute(one, "tensor", [(t, t ^ 1) for t in range(shards)])
    normed, extra = normalise(one, two)
    for s in range(2, ring // 2):
        a, b = turn(a, b, s)
        chunks += [a, b]
    last, _ = turn(a, b, ring // 2)
    aheads = [0] + [s if i else -s for s in range(1, ring // 2 + 1) for i in range(2)]
    acc = accumulate(aheads[0:9], normed, chunks[0:9])
    acc = accumulate(aheads[9:15], normed, chunks[9:15], acc)
    flags = extra[:, :, 1:3, :share].transpose(2, 1, 0, 3).reshape(2, 1, tokens)
    seq, alive = flags[0].astype(jnp.int32), flags[1]
    stats = statistics(ring // 2, normed, last, acc, targets)

    everyone = lax.all_to_all(
        jnp.broadcast_to(stats[None], (shards, *stats.shape)), "tensor", 0, 0
    )
    logprob, entropy, sums = combine(everyone, seq, alive)
    planes = lax.all_to_all(jnp.broadcast_to(sums, (ring, 2 * SEQS)), "dp", 0, 0)
    whole = jnp.sum(planes, axis=0)
    seq_mean = whole[:SEQS] / jnp.maximum(whole[SEQS:], 1.0)
    return logprob[0], entropy[0], seq_mean


def solution(mesh):
    placed = (
        P("dp", "tensor"),
        P("tensor"),
        P("dp", "tensor"),
        P("dp"),
        P(("dp", "tensor")),
        P(("dp", "tensor")),
    )

    return jax.shard_map(
        body,
        mesh=mesh,
        in_specs=placed,
        out_specs=(P(("dp", "tensor")), P(("dp", "tensor")), P()),
        check_vma=False,
    )
```

time: 200 us -> 229 us (1.15)
  blocking collectives: 0 us -> 69.1 us
  starting transfers between devices: 86.6 us -> 69.5 us
  waiting for transfers between devices: 75.5 us -> 63.3 us
  Pallas kernels: 25.7 us -> 20.5 us
  local copies, waits for them, and re-layouts: 8.8 us -> 4.01 us
    all_to_all x0 -> x2, blocking collectives: none -> 69.1 us  [the longest x1 50.6 us: body(): one = lax.all_to_all(sent, 'tensor', 0, 0, axis_index_groups=teams)]
    ppermute x7, waiting for transfers between devices: 29.1 us -> 0.02 us  [turn(): b = lax.ppermute(b, 'dp', back)]
    ppermute x8, waiting for transfers between devices: 25.2 us -> 52.5 us  [turn(): a = lax.ppermute(a, 'dp', forth)]
    all_to_all x2 -> x0, starting transfers between devices: 14 us -> none  [the longest x1 7.75 us: body(): one = lax.all_to_all(sent, 'tensor', 0, 0, axis_index_groups=teams)]
    all_to_all x2 -> x0, waiting for transfers between devices: 10.7 us -> none  [the longest x1 10.7 us: body(): lax.all_to_all(jnp.broadcast_to(sums, (ring, 2 * SEQS)), 'dp', 0, 0)]
    pallas_call x5, Pallas kernels: 25 us -> 18.9 us  [the longest x2 8.42 us: accumulate(): pl.pallas_call(functools.partial(mm_kernel, tuple(aheads)), out_shape=jax...]
    ppermute x7, starting transfers between devices: 41.8 us -> 36.9 us  [turn(): b = lax.ppermute(b, 'dp', back)]
    unnamed x22 -> x12, local copies, waits for them, and re-layouts: 6.31 us -> 2.91 us
  transfers between devices with their start and end apart: 19 -> 17, of which waited for: 13 -> 8; matrix products, arithmetic and copies ran while one was open for 1% -> 0% of each run, Pallas kernels for 9% -> 6%
where the time goes in v2:
time: 229 us; the launch traced here: 228 us
  starting transfers between devices  69.5 us (30%)
  blocking collectives  69.1 us (30%)
  waiting for transfers between devices  63.3 us (28%)
  Pallas kernels  20.5 us (9%)
  local copies, waits for them, and re-layouts  4.01 us (2%)
    ppermute x8, waiting for transfers between devices, turn(): a = lax.ppermute(a, 'dp', forth)  52.5 us
    all_to_all x1, blocking collectives, body(): one = lax.all_to_all(sent, 'tensor', 0, 0, axis_index_groups=teams)  50.6 us
    ppermute x7, starting transfers between devices, turn(): b = lax.ppermute(b, 'dp', back)  36.9 us
    all_to_all x1, blocking collectives, body(): lax.all_to_all(jnp.broadcast_to(sums, (ring, 2 * SEQS)), 'dp', 0, 0)  18.6 us
    ppermute x8, starting transfers between devices, turn(): a = lax.ppermute(a, 'dp', forth)  17.4 us
    all_to_all x1, waiting for transfers between devices, body(): lax.all_to_all(jnp.broadcast_to(stats[None], (shards, *stats.shape)), 'te...  10.7 us
    all_to_all x1, starting transfers between devices, body(): lax.all_to_all(jnp.broadcast_to(stats[None], (shards, *stats.shape)), 'te...  9.26 us
    pallas_call x2, Pallas kernels, accumulate(): pl.pallas_call(functools.partial(mm_kernel, tuple(aheads)), out_shape=jax...  8.42 us
  transfers between devices with their start and end apart: 17, of which 8 were waited for; matrix products, arithmetic and copies ran while one was open for 0% of the time, Pallas kernels for 6%

profile of v2, /device:TPU:1, one launch (start us, length us, event | category | flops | bytes accessed | tf_op | source)
XLA Modules:
  0.0 228.0 jit_solution(10766191472607766430)
XLA Ops:
  0.6 0.0 copy-start.1
  0.6 0.9 copy-done.1
  1.6 0.0 copy-start.3
  1.6 0.7 copy-done.3
  2.2 0.0 copy-start.4
  2.2 0.7 copy-done.4
  2.9 0.0 copy-start.5
  2.9 0.7 copy-done.5
  3.5 2.2 fan.1
  5.8 0.0 copy-start
  5.8 50.6 %all_to_all.16.one_ref.gain_one_ref = bf16[16,912,128]{2,1,0:T(8,128)(2,1)S(1)} all-to-all(bf16[16,912,128]{2,1,0:T(8,128)(2,1)} %fan.1), channel_id=1, replica_groups={{0,2,4,6,8,10,12,14,16,18,20,22,24,26,28,30},{1,3,5,7,9,11,13,15,17,19,..., dimensions={0} | all-to-all | bytes 7471104 | tf_op jit(solution)/shard_map/all_to_all | solution.py:261
  56.4 5.9 %collective-permute-start = (bf16[16,912,128]{2,1,0:T(8,128)(2,1)S(1)}, bf16[16,912,128]{2,1,0:T(8,128)(2,1)S(1)}, u32[]{:S(2)}, u32[]{:S(2)}) collective-permute-start(bf16[16,912,128]{2,1,0:T(8,128)(2,1)S(1)} %all_to_all.16.one_ref.gain_one_ref), channel_id=1, source_target_pairs={{0,1},{1,0},{2,3},{3,2},{4,5},{5,4},{6,7},{7,6},{8,9},{9,8},{10,11... | collective-permute-start | bytes 11206664 | tf_op jit(solution)/shard_map/ppermute | solution.py:262
  62.3 0.0 copy-done
  62.3 4.1 %collective-permute-start.1 = (bf16[1000,256]{1,0:T(8,128)(2,1)S(1)}, bf16[1000,256]{1,0:T(8,128)(2,1)S(1)}, u32[]{:S(2)}, u32[]{:S(2)}) collective-permute-start(bf16[1000,256]{1,0:T(8,128)(2,1)S(1)} %bitcast.10), channel_id=1, source_target_pairs={{0,32},{32,64},{64,96},{96,128},{128,160},{160,192},{192,224},{224... | collective-permute-start | bytes 1536008 | tf_op jit(solution)/shard_map/ppermute | solution.py:251
  66.4 9.5 %collective-permute-start.9 = (bf16[1000,256]{1,0:T(8,128)(2,1)S(1)}, bf16[1000,256]{1,0:T(8,128)(2,1)S(1)}, u32[]{:S(2)}, u32[]{:S(2)}) collective-permute-start(bf16[1000,256]{1,0:T(8,128)(2,1)S(1)} %bitcast.11), channel_id=1, source_target_pairs={{0,480},{32,0},{64,32},{96,64},{128,96},{160,128},{192,160},{224,1... | collective-permute-start | bytes 1536008 | tf_op jit(solution)/shard_map/ppermute | solution.py:253
  75.9 10.1 %collective-permute-done.1.refs_1_ = bf16[1000,256]{1,0:T(8,128)(2,1)S(1)} collective-permute-done((bf16[1000,256]{1,0:T(8,128)(2,1)S(1)}, bf16[1000,256]{1,0:T(8,128)(2,1)S(1)}, u32[]{:S(2)}, u32[]{:S(2)}) %collective-permute-start.1) | collective-permute-done | bytes 512032 | tf_op jit(solution)/shard_map/ppermute | solution.py:251
  86.0 1.9 collective-permute-start.2
  87.9 0.0 collective-permute-done.9.refs_2_
  87.9 4.6 %collective-permute-start.10 = (bf16[1000,256]{1,0:T(8,128)(2,1)S(1)}, bf16[1000,256]{1,0:T(8,128)(2,1)S(1)}, u32[]{:S(2)}, u32[]{:S(2)}) collective-permute-start(bf16[1000,256]{1,0:T(8,128)(2,1)S(1)} %collective-permute-done.9.refs_2_), channel_id=1, source_target_pairs={{0,480},{32,0},{64,32},{96,64},{128,96},{160,128},{192,160},{224,1... | collective-permute-start | bytes 1536008 | tf_op jit(solution)/shard_map/ppermute | solution.py:253
  92.5 9.2 %collective-permute-done.2.refs_3_ = bf16[1000,256]{1,0:T(8,128)(2,1)S(1)} collective-permute-done((bf16[1000,256]{1,0:T(8,128)(2,1)S(1)}, bf16[1000,256]{1,0:T(8,128)(2,1)S(1)}, u32[]{:S(2)}, u32[]{:S(2)}) %collective-permute-start.2) | collective-permute-done | bytes 512032 | tf_op jit(solution)/shard_map/ppermute | solution.py:251
  101.7 1.9 collective-permute-start.3
  103.6 0.0 collective-permute-done.10.refs_4_
  103.6 4.6 %collective-permute-start.11 = (bf16[1000,256]{1,0:T(8,128)(2,1)S(1)}, bf16[1000,256]{1,0:T(8,128)(2,1)S(1)}, u32[]{:S(2)}, u32[]{:S(2)}) collective-permute-start(bf16[1000,256]{1,0:T(8,128)(2,1)S(1)} %collective-permute-done.10.refs_4_), channel_id=1, source_target_pairs={{0,480},{32,0},{64,32},{96,64},{128,96},{160,128},{192,160},{224,1... | collective-permute-start | bytes 1536008 | tf_op jit(solution)/shard_map/ppermute | solution.py:253
  108.2 8.4 %collective-permute-done.3.refs_5_ = bf16[1000,256]{1,0:T(8,128)(2,1)S(1)} collective-permute-done((bf16[1000,256]{1,0:T(8,128)(2,1)S(1)}, bf16[1000,256]{1,0:T(8,128)(2,1)S(1)}, u32[]{:S(2)}, u32[]{:S(2)}) %collective-permute-start.3) | collective-permute-done | bytes 512032 | tf_op jit(solution)/shard_map/ppermute | solution.py:251
  116.6 1.9 collective-permute-start.4
  118.5 0.0 collective-permute-done.11.refs_6_
  118.5 4.6 %collective-permute-start.12 = (bf16[1000,256]{1,0:T(8,128)(2,1)S(1)}, bf16[1000,256]{1,0:T(8,128)(2,1)S(1)}, u32[]{:S(2)}, u32[]{:S(2)}) collective-permute-start(bf16[1000,256]{1,0:T(8,128)(2,1)S(1)} %collective-permute-done.11.refs_6_), channel_id=1, source_target_pairs={{0,480},{32,0},{64,32},{96,64},{128,96},{160,128},{192,160},{224,1... | collective-permute-start | bytes 1536008 | tf_op jit(solution)/shard_map/ppermute | solution.py:253
  123.1 7.5 %collective-permute-done.4.refs_7_ = bf16[1000,256]{1,0:T(8,128)(2,1)S(1)} collective-permute-done((bf16[1000,256]{1,0:T(8,128)(2,1)S(1)}, bf16[1000,256]{1,0:T(8,128)(2,1)S(1)}, u32[]{:S(2)}, u32[]{:S(2)}) %collective-permute-start.4) | collective-permute-done | bytes 512032 | tf_op jit(solution)/shard_map/ppermute | solution.py:251
  130.6 1.9 collective-permute-start.5
  132.5 0.0 collective-permute-done.12.refs_8_
  132.5 4.6 %collective-permute-start.13 = (bf16[1000,256]{1,0:T(8,128)(2,1)S(1)}, bf16[1000,256]{1,0:T(8,128)(2,1)S(1)}, u32[]{:S(2)}, u32[]{:S(2)}) collective-permute-start(bf16[1000,256]{1,0:T(8,128)(2,1)S(1)} %collective-permute-done.12.refs_8_), channel_id=1, source_target_pairs={{0,480},{32,0},{64,32},{96,64},{128,96},{160,128},{192,160},{224,1... | collective-permute-start | bytes 1536008 | tf_op jit(solution)/shard_map/ppermute | solution.py:253
  137.1 6.6 %collective-permute-done.5.refs_0_ = bf16[1000,256]{1,0:T(8,128)(2,1)S(1)} collective-permute-done((bf16[1000,256]{1,0:T(8,128)(2,1)S(1)}, bf16[1000,256]{1,0:T(8,128)(2,1)S(1)}, u32[]{:S(2)}, u32[]{:S(2)}) %collective-permute-start.5) | collective-permute-done | bytes 512032 | tf_op jit(solution)/shard_map/ppermute | solution.py:251
  143.7 1.9 collective-permute-start.6
  145.6 0.0 collective-permute-done.13.refs_1_
  145.7 4.6 %collective-permute-start.14 = (bf16[1000,256]{1,0:T(8,128)(2,1)S(1)}, bf16[1000,256]{1,0:T(8,128)(2,1)S(1)}, u32[]{:S(2)}, u32[]{:S(2)}) collective-permute-start(bf16[1000,256]{1,0:T(8,128)(2,1)S(1)} %collective-permute-done.13.refs_1_), channel_id=1, source_target_pairs={{0,480},{32,0},{64,32},{96,64},{128,96},{160,128},{192,160},{224,1... | collective-permute-start | bytes 1536008 | tf_op jit(solution)/shard_map/ppermute | solution.py:253
  150.2 5.8 %collective-permute-done.6.refs_2_ = bf16[1000,256]{1,0:T(8,128)(2,1)S(1)} collective-permute-done((bf16[1000,256]{1,0:T(8,128)(2,1)S(1)}, bf16[1000,256]{1,0:T(8,128)(2,1)S(1)}, u32[]{:S(2)}, u32[]{:S(2)}) %collective-permute-start.6) | collective-permute-done | bytes 512032 | tf_op jit(solution)/shard_map/ppermute | solution.py:251
  156.0 1.9 collective-permute-start.7
  157.9 0.0 collective-permute-done.14.refs_3_
  158.0 4.6 %collective-permute-start.15 = (bf16[1000,256]{1,0:T(8,128)(2,1)S(1)}, bf16[1000,256]{1,0:T(8,128)(2,1)S(1)}, u32[]{:S(2)}, u32[]{:S(2)}) collective-permute-start(bf16[1000,256]{1,0:T(8,128)(2,1)S(1)} %collective-permute-done.14.refs_3_), channel_id=1, source_target_pairs={{0,480},{32,0},{64,32},{96,64},{128,96},{160,128},{192,160},{224,1... | collective-permute-start | bytes 1536008 | tf_op jit(solution)/shard_map/ppermute | solution.py:253
  162.5 4.9 %collective-permute-done.7.refs_4_ = bf16[1000,256]{1,0:T(8,128)(2,1)S(1)} collective-permute-done((bf16[1000,256]{1,0:T(8,128)(2,1)S(1)}, bf16[1000,256]{1,0:T(8,128)(2,1)S(1)}, u32[]{:S(2)}, u32[]{:S(2)}) %collective-permute-start.7) | collective-permute-done | bytes 512032 | tf_op jit(solution)/shard_map/ppermute | solution.py:251
  167.5 1.9 collective-permute-start.8
  169.4 0.0 collective-permute-done.two_ref.gain_two_ref
  169.4 6.4 %norm.1 = (bf16[16,896,256]{2,1,0:T(8,128)(2,1)S(1)}, f32[2,16,16,128]{3,2,1,0:T(8,128)S(1)}) custom-call(bf16[16,912,128]{2,1,0:T(8,128)(2,1)S(1)} %all_to_all.16.one_ref.gain_one_ref, bf16[16,912,128]{2,1,0:T(8,128)(2,1)S(1)} %collective-permute-done.two_ref.gain_two_ref, bf16[16,912,128]{2,1,0:T(8,128)(2,1)S(1)} %all_to_all.16.one_ref.gain_one_ref, ...), custom_call_target="tpu_custom_call" | custom-call | flops 22413312 | bytes 14942208 | tf_op jit(solution)/shard_map/norm/pallas_call | solution.py:99
  175.8 5.0 %scores.2.refs_6_ = f32[1000,896]{1,0:T(8,128)S(1)} custom-call(bf16[16,896,256]{2,1,0:T(8,128)(2,1)S(1)} %get-tuple-element.8.n_ref, bf16[1000,256]{1,0:T(8,128)(2,1)S(1)} %bitcast.12, bf16[1000,256]{1,0:T(8,128)(2,1)S(1)} %collective-permute-done.1.refs_1_, bf16[1000,256]{1,0:T(8,128)(2,1)S(1)} %collective-permute-done.9.refs_2_, ...), custom_call_target="tpu_custom_call" | custom-call | flops 4128768000 | bytes 7168000 | tf_op jit(solution)/shard_map/scores/pallas_call | solution.py:145
  180.8 0.0 copy-start.2
  180.8 0.0 collective-permute-done.15.refs_5_
  180.8 3.4 %scores.3.acc_ref = f32[1000,896]{1,0:T(8,128)S(1)} custom-call(bf16[16,896,256]{2,1,0:T(8,128)(2,1)S(1)} %get-tuple-element.8.n_ref, bf16[1000,256]{1,0:T(8,128)(2,1)S(1)} %collective-permute-done.5.refs_0_, bf16[1000,256]{1,0:T(8,128)(2,1)S(1)} %collective-permute-done.13.refs_1_, ...), custom_call_target="tpu_custom_call", output_to_operand_aliasing={{}: (7, {})} | custom-call | flops 2752512000 | bytes 7168000 | tf_op jit(solution)/shard_map/scores/pallas_call | solution.py:145
  184.2 0.0 collective-permute-done.8.w_ref
  184.2 0.0 copy-done.2
  184.3 1.9 stats.1
  186.1 0.8 broadcast_in_dim.23
  186.9 9.3 %all-to-all-start.1 = ((f32[32,4,896]{2,1,0:T(4,128)}), f32[32,4,896]{2,1,0:T(4,128)S(1)}, u32[]{:S(2)}, u32[]{:S(2)}) async-start(f32[32,4,896]{2,1,0:T(4,128)} %broadcast_in_dim.23), calls=%async_computation.1 | async-start | bytes 917504 | tf_op jit(solution)/shard_map/all_to_all | solution.py:275
  196.3 0.1 convert_element_type.6.seq_ref
  196.4 0.1 squeeze.10.live_ref
  196.5 10.7 %all-to-all-done.1.x_ref = f32[32,4,896]{2,1,0:T(4,128)S(1)} async-done(((f32[32,4,896]{2,1,0:T(4,128)}), f32[32,4,896]{2,1,0:T(4,128)S(1)}, u32[]{:S(2)}, u32[]{:S(2)}) %all-to-all-start.1) | async-done | bytes 458784 | tf_op jit(solution)/shard_map/all_to_all | solution.py:275
  207.3 1.6 combine.1
  208.9 18.6 %all_to_all.17 = f32[16,1,128]{2,1,0:T(1,128)S(1)} all-to-all(f32[16,1,128]{2,1,0:T(1,128)S(1)} %broadcast_in_dim.24), channel_id=1, replica_groups=mesh['dp'=16,'tensor'=32] {'dp'}, dimensions={0} | all-to-all | bytes 16384 | tf_op jit(solution)/shard_map/all_to_all | solution.py:279
  227.4 0.6 maximum_divide_fusion
  (6 shorter events, 0.1 us)
Async XLA Ops:
  0.6 0.9 copy-start.1
  1.6 0.7 copy-start.3
  2.2 0.7 copy-start.4
  2.9 0.7 copy-start.5
  5.8 56.5 %copy-start = (bf16[256,1000]{0,1:T(8,128)(2,1)S(1)}, bf16[256,1000]{0,1:T(8,128)(2,1)}, u32[]{:S(2)}) copy-start(bf16[256,1000]{0,1:T(8,128)(2,1)} %param.8) | copy-start | bytes 1536004
  56.4 113.0 %collective-permute-start = (bf16[16,912,128]{2,1,0:T(8,128)(2,1)S(1)}, bf16[16,912,128]{2,1,0:T(8,128)(2,1)S(1)}, u32[]{:S(2)}, u32[]{:S(2)}) collective-permute-start(bf16[16,912,128]{2,1,0:T(8,128)(2,1)S(1)} %all_to_all.16.one_ref.gain_one_ref), channel_id=1, source_target_pairs={{0,1},{1,0},{2,3},{3,2},{4,5},{5,4},{6,7},{7,6},{8,9},{9,8},{10,11... | collective-permute-start | bytes 11206664 | tf_op jit(solution)/shard_map/ppermute | solution.py:262
  62.3 23.7 %collective-permute-start.1 = (bf16[1000,256]{1,0:T(8,128)(2,1)S(1)}, bf16[1000,256]{1,0:T(8,128)(2,1)S(1)}, u32[]{:S(2)}, u32[]{:S(2)}) collective-permute-start(bf16[1000,256]{1,0:T(8,128)(2,1)S(1)} %bitcast.10), channel_id=1, source_target_pairs={{0,32},{32,64},{64,96},{96,128},{128,160},{160,192},{192,224},{224... | collective-permute-start | bytes 1536008 | tf_op jit(solution)/shard_map/ppermute | solution.py:251
  66.4 21.5 %collective-permute-start.9 = (bf16[1000,256]{1,0:T(8,128)(2,1)S(1)}, bf16[1000,256]{1,0:T(8,128)(2,1)S(1)}, u32[]{:S(2)}, u32[]{:S(2)}) collective-permute-start(bf16[1000,256]{1,0:T(8,128)(2,1)S(1)} %bitcast.11), channel_id=1, source_target_pairs={{0,480},{32,0},{64,32},{96,64},{128,96},{160,128},{192,160},{224,1... | collective-permute-start | bytes 1536008 | tf_op jit(solution)/shard_map/ppermute | solution.py:253
  86.0 15.7 %collective-permute-start.2 = (bf16[1000,256]{1,0:T(8,128)(2,1)S(1)}, bf16[1000,256]{1,0:T(8,128)(2,1)S(1)}, u32[]{:S(2)}, u32[]{:S(2)}) collective-permute-start(bf16[1000,256]{1,0:T(8,128)(2,1)S(1)} %collective-permute-done.1.refs_1_), channel_id=1, source_target_pairs={{0,32},{32,64},{64,96},{96,128},{128,160},{160,192},{192,224},{224... | collective-permute-start | bytes 1536008 | tf_op jit(solution)/shard_map/ppermute | solution.py:251
  87.9 15.7 %collective-permute-start.10 = (bf16[1000,256]{1,0:T(8,128)(2,1)S(1)}, bf16[1000,256]{1,0:T(8,128)(2,1)S(1)}, u32[]{:S(2)}, u32[]{:S(2)}) collective-permute-start(bf16[1000,256]{1,0:T(8,128)(2,1)S(1)} %collective-permute-done.9.refs_2_), channel_id=1, source_target_pairs={{0,480},{32,0},{64,32},{96,64},{128,96},{160,128},{192,160},{224,1... | collective-permute-start | bytes 1536008 | tf_op jit(solution)/shard_map/ppermute | solution.py:253
  101.7 14.9 %collective-permute-start.3 = (bf16[1000,256]{1,0:T(8,128)(2,1)S(1)}, bf16[1000,256]{1,0:T(8,128)(2,1)S(1)}, u32[]{:S(2)}, u32[]{:S(2)}) collective-permute-start(bf16[1000,256]{1,0:T(8,128)(2,1)S(1)} %collective-permute-done.2.refs_3_), channel_id=1, source_target_pairs={{0,32},{32,64},{64,96},{96,128},{128,160},{160,192},{192,224},{224... | collective-permute-start | bytes 1536008 | tf_op jit(solution)/shard_map/ppermute | solution.py:251
  103.6 14.9 %collective-permute-start.11 = (bf16[1000,256]{1,0:T(8,128)(2,1)S(1)}, bf16[1000,256]{1,0:T(8,128)(2,1)S(1)}, u32[]{:S(2)}, u32[]{:S(2)}) collective-permute-start(bf16[1000,256]{1,0:T(8,128)(2,1)S(1)} %collective-permute-done.10.refs_4_), channel_id=1, source_target_pairs={{0,480},{32,0},{64,32},{96,64},{128,96},{160,128},{192,160},{224,1... | collective-permute-start | bytes 1536008 | tf_op jit(solution)/shard_map/ppermute | solution.py:253
  116.6 14.0 %collective-permute-start.4 = (bf16[1000,256]{1,0:T(8,128)(2,1)S(1)}, bf16[1000,256]{1,0:T(8,128)(2,1)S(1)}, u32[]{:S(2)}, u32[]{:S(2)}) collective-permute-start(bf16[1000,256]{1,0:T(8,128)(2,1)S(1)} %collective-permute-done.3.refs_5_), channel_id=1, source_target_pairs={{0,32},{32,64},{64,96},{96,128},{128,160},{160,192},{192,224},{224... | collective-permute-start | bytes 1536008 | tf_op jit(solution)/shard_map/ppermute | solution.py:251
  118.5 14.0 %collective-permute-start.12 = (bf16[1000,256]{1,0:T(8,128)(2,1)S(1)}, bf16[1000,256]{1,0:T(8,128)(2,1)S(1)}, u32[]{:S(2)}, u32[]{:S(2)}) collective-permute-start(bf16[1000,256]{1,0:T(8,128)(2,1)S(1)} %collective-permute-done.11.refs_6_), channel_id=1, source_target_pairs={{0,480},{32,0},{64,32},{96,64},{128,96},{160,128},{192,160},{224,1... | collective-permute-start | bytes 1536008 | tf_op jit(solution)/shard_map/ppermute | solution.py:253
  130.6 13.2 %collective-permute-start.5 = (bf16[1000,256]{1,0:T(8,128)(2,1)S(1)}, bf16[1000,256]{1,0:T(8,128)(2,1)S(1)}, u32[]{:S(2)}, u32[]{:S(2)}) collective-permute-start(bf16[1000,256]{1,0:T(8,128)(2,1)S(1)} %collective-permute-done.4.refs_7_), channel_id=1, source_target_pairs={{0,32},{32,64},{64,96},{96,128},{128,160},{160,192},{192,224},{224... | collective-permute-start | bytes 1536008 | tf_op jit(solution)/shard_map/ppermute | solution.py:251
  132.5 13.1 %collective-permute-start.13 = (bf16[1000,256]{1,0:T(8,128)(2,1)S(1)}, bf16[1000,256]{1,0:T(8,128)(2,1)S(1)}, u32[]{:S(2)}, u32[]{:S(2)}) collective-permute-start(bf16[1000,256]{1,0:T(8,128)(2,1)S(1)} %collective-permute-done.12.refs_8_), channel_id=1, source_target_pairs={{0,480},{32,0},{64,32},{96,64},{128,96},{160,128},{192,160},{224,1... | collective-permute-start | bytes 1536008 | tf_op jit(solution)/shard_map/ppermute | solution.py:253
  143.7 12.3 %collective-permute-start.6 = (bf16[1000,256]{1,0:T(8,128)(2,1)S(1)}, bf16[1000,256]{1,0:T(8,128)(2,1)S(1)}, u32[]{:S(2)}, u32[]{:S(2)}) collective-permute-start(bf16[1000,256]{1,0:T(8,128)(2,1)S(1)} %collective-permute-done.5.refs_0_), channel_id=1, source_target_pairs={{0,32},{32,64},{64,96},{96,128},{128,160},{160,192},{192,224},{224... | collective-permute-start | bytes 1536008 | tf_op jit(solution)/shard_map/ppermute | solution.py:251
  145.7 12.3 %collective-permute-start.14 = (bf16[1000,256]{1,0:T(8,128)(2,1)S(1)}, bf16[1000,256]{1,0:T(8,128)(2,1)S(1)}, u32[]{:S(2)}, u32[]{:S(2)}) collective-permute-start(bf16[1000,256]{1,0:T(8,128)(2,1)S(1)} %collective-permute-done.13.refs_1_), channel_id=1, source_target_pairs={{0,480},{32,0},{64,32},{96,64},{128,96},{160,128},{192,160},{224,1... | collective-permute-start | bytes 1536008 | tf_op jit(solution)/shard_map/ppermute | solution.py:253
  156.0 11.4 %collective-permute-start.7 = (bf16[1000,256]{1,0:T(8,128)(2,1)S(1)}, bf16[1000,256]{1,0:T(8,128)(2,1)S(1)}, u32[]{:S(2)}, u32[]{:S(2)}) collective-permute-start(bf16[1000,256]{1,0:T(8,128)(2,1)S(1)} %collective-permute-done.6.refs_2_), channel_id=1, source_target_pairs={{0,32},{32,64},{64,96},{96,128},{128,160},{160,192},{192,224},{224... | collective-permute-start | bytes 1536008 | tf_op jit(solution)/shard_map/ppermute | solution.py:251
  158.0 22.8 %collective-permute-start.15 = (bf16[1000,256]{1,0:T(8,128)(2,1)S(1)}, bf16[1000,256]{1,0:T(8,128)(2,1)S(1)}, u32[]{:S(2)}, u32[]{:S(2)}) collective-permute-start(bf16[1000,256]{1,0:T(8,128)(2,1)S(1)} %collective-permute-done.14.refs_3_), channel_id=1, source_target_pairs={{0,480},{32,0},{64,32},{96,64},{128,96},{160,128},{192,160},{224,1... | collective-permute-start | bytes 1536008 | tf_op jit(solution)/shard_map/ppermute | solution.py:253
  167.5 16.8 %collective-permute-start.8 = (bf16[1000,256]{1,0:T(8,128)(2,1)S(1)}, bf16[1000,256]{1,0:T(8,128)(2,1)S(1)}, u32[]{:S(2)}, u32[]{:S(2)}) collective-permute-start(bf16[1000,256]{1,0:T(8,128)(2,1)S(1)} %collective-permute-done.7.refs_4_), channel_id=1, source_target_pairs={{0,32},{32,64},{64,96},{96,128},{128,160},{160,192},{192,224},{224... | collective-permute-start | bytes 1536008 | tf_op jit(solution)/shard_map/ppermute | solution.py:251
  180.8 3.5 %copy-start.2 = (s32[896]{0:T(1024)S(1)}, s32[896]{0:T(1024)}, u32[]{:S(2)}) copy-start(s32[896]{0:T(1024)} %ids_ref.1) | copy-start | bytes 10756
  186.9 20.3 %all-to-all-start.1 = ((f32[32,4,896]{2,1,0:T(4,128)}), f32[32,4,896]{2,1,0:T(4,128)S(1)}, u32[]{:S(2)}, u32[]{:S(2)}) async-start(f32[32,4,896]{2,1,0:T(4,128)} %broadcast_in_dim.23), calls=%async_computation.1 | async-start | bytes 917504 | tf_op jit(solution)/shard_map/all_to_all | solution.py:275

commit v3 on v2

--- a/solution.py
+++ b/solution.py
@@ -65,7 +65,7 @@
         ],
         compiler_params=room(4),
         name="fan",
-    )(hidden, gain[None], seq_ids[None], live[None])
+    )(*(pltpu.with_memory_space_constraint(x, pltpu.HBM) for x in (hidden, gain[None], seq_ids[None], live[None])))
 
 
 def norm_kernel(one_ref, two_ref, gain_one_ref, gain_two_ref, out_ref, flag_ref):
@@ -266,8 +266,8 @@
         chunks += [a, b]
     last, _ = turn(a, b, ring // 2)
     aheads = [0] + [s if i else -s for s in range(1, ring // 2 + 1) for i in range(2)]
-    acc = accumulate(aheads[0:9], normed, chunks[0:9])
-    acc = accumulate(aheads[9:15], normed, chunks[9:15], acc)
+    acc = accumulate(aheads[0:7], normed, chunks[0:7])
+    acc = accumulate(aheads[7:15], normed, chunks[7:15], acc)
     flags = extra[:, :, 1:3, :share].transpose(2, 1, 0, 3).reshape(2, 1, tokens)
     seq, alive = flags[0].astype(jnp.int32), flags[1]
     stats = statistics(ring // 2, normed, last, acc, targets)

time: 229 us -> 227 us (level)
  local copies, waits for them, and re-layouts: 4.01 us -> 1.12 us
    unnamed x12 -> x4, local copies, waits for them, and re-layouts: 2.91 us -> 0.01 us
  transfers between devices with their start and end apart: 17 -> 17, of which waited for: 8 -> 8; matrix products, arithmetic and copies ran while one was open for 0% -> 0% of each run, Pallas kernels for 6% -> 7%
where the time goes in v3:
time: 227 us; the launch traced here: 226 us
  starting transfers between devices  69.5 us (31%)
  blocking collectives  69.1 us (30%)
  waiting for transfers between devices  63.3 us (28%)
  Pallas kernels  21.2 us (9%)
    ppermute x8, waiting for transfers between devices, turn(): a = lax.ppermute(a, 'dp', forth)  52.5 us
    all_to_all x1, blocking collectives, body(): one = lax.all_to_all(sent, 'tensor', 0, 0, axis_index_groups=teams)  50.6 us
    ppermute x7, starting transfers between devices, turn(): b = lax.ppermute(b, 'dp', back)  36.9 us
    all_to_all x1, blocking collectives, body(): lax.all_to_all(jnp.broadcast_to(sums, (ring, 2 * SEQS)), 'dp', 0, 0)  18.6 us
    ppermute x8, starting transfers between devices, turn(): a = lax.ppermute(a, 'dp', forth)  17.4 us
    all_to_all x1, waiting for transfers between devices, body(): lax.all_to_all(jnp.broadcast_to(stats[None], (shards, *stats.shape)), 'te...  10.7 us
    all_to_all x1, starting transfers between devices, body(): lax.all_to_all(jnp.broadcast_to(stats[None], (shards, *stats.shape)), 'te...  9.26 us
    pallas_call x2, Pallas kernels, accumulate(): pl.pallas_call(functools.partial(mm_kernel, tuple(aheads)), out_shape=jax...  8.42 us
  transfers between devices with their start and end apart: 17, of which 8 were waited for; matrix products, arithmetic and copies ran while one was open for 0% of the time, Pallas kernels for 7%

profile of v3, /device:TPU:1, one launch (start us, length us, event | category | flops | bytes accessed | tf_op | source)
XLA Modules:
  0.0 225.8 jit_solution(13616502930507535969)
XLA Ops:
  0.6 2.9 %fan.1 = bf16[16,912,128]{2,1,0:T(8,128)(2,1)} custom-call(bf16[896,128]{1,0:T(8,128)(2,1)} %hid_ref.1, bf16[1,128]{1,0:T(2,128)(2,1)} %bitcast.15, s32[1,28]{1,0:T(1,128)} %bitcast.16, s32[1,28]{1,0:T(1,128)} %bitcast.17), custom_call_target="tpu_custom_call" | custom-call | tf_op jit(solution)/shard_map/fan/pallas_call | solution.py:53
  3.6 0.0 copy-start
  3.6 50.6 %all_to_all.16.one_ref.gain_one_ref = bf16[16,912,128]{2,1,0:T(8,128)(2,1)S(1)} all-to-all(bf16[16,912,128]{2,1,0:T(8,128)(2,1)} %fan.1), channel_id=1, replica_groups={{0,2,4,6,8,10,12,14,16,18,20,22,24,26,28,30},{1,3,5,7,9,11,13,15,17,19,..., dimensions={0} | all-to-all | bytes 7471104 | tf_op jit(solution)/shard_map/all_to_all | solution.py:261
  54.2 5.9 %collective-permute-start = (bf16[16,912,128]{2,1,0:T(8,128)(2,1)S(1)}, bf16[16,912,128]{2,1,0:T(8,128)(2,1)S(1)}, u32[]{:S(2)}, u32[]{:S(2)}) collective-permute-start(bf16[16,912,128]{2,1,0:T(8,128)(2,1)S(1)} %all_to_all.16.one_ref.gain_one_ref), channel_id=1, source_target_pairs={{0,1},{1,0},{2,3},{3,2},{4,5},{5,4},{6,7},{7,6},{8,9},{9,8},{10,11... | collective-permute-start | bytes 11206664 | tf_op jit(solution)/shard_map/ppermute | solution.py:262
  60.1 0.0 copy-done
  60.1 4.1 %collective-permute-start.1 = (bf16[1000,256]{1,0:T(8,128)(2,1)S(1)}, bf16[1000,256]{1,0:T(8,128)(2,1)S(1)}, u32[]{:S(2)}, u32[]{:S(2)}) collective-permute-start(bf16[1000,256]{1,0:T(8,128)(2,1)S(1)} %bitcast.10), channel_id=1, source_target_pairs={{0,32},{32,64},{64,96},{96,128},{128,160},{160,192},{192,224},{224... | collective-permute-start | bytes 1536008 | tf_op jit(solution)/shard_map/ppermute | solution.py:251
  64.2 9.5 %collective-permute-start.9 = (bf16[1000,256]{1,0:T(8,128)(2,1)S(1)}, bf16[1000,256]{1,0:T(8,128)(2,1)S(1)}, u32[]{:S(2)}, u32[]{:S(2)}) collective-permute-start(bf16[1000,256]{1,0:T(8,128)(2,1)S(1)} %bitcast.11), channel_id=1, source_target_pairs={{0,480},{32,0},{64,32},{96,64},{128,96},{160,128},{192,160},{224,1... | collective-permute-start | bytes 1536008 | tf_op jit(solution)/shard_map/ppermute | solution.py:253
  73.7 10.1 %collective-permute-done.1.refs_1_ = bf16[1000,256]{1,0:T(8,128)(2,1)S(1)} collective-permute-done((bf16[1000,256]{1,0:T(8,128)(2,1)S(1)}, bf16[1000,256]{1,0:T(8,128)(2,1)S(1)}, u32[]{:S(2)}, u32[]{:S(2)}) %collective-permute-start.1) | collective-permute-done | bytes 512032 | tf_op jit(solution)/shard_map/ppermute | solution.py:251
  83.8 1.9 collective-permute-start.2
  85.7 0.0 collective-permute-done.9.refs_2_
  85.7 4.6 %collective-permute-start.10 = (bf16[1000,256]{1,0:T(8,128)(2,1)S(1)}, bf16[1000,256]{1,0:T(8,128)(2,1)S(1)}, u32[]{:S(2)}, u32[]{:S(2)}) collective-permute-start(bf16[1000,256]{1,0:T(8,128)(2,1)S(1)} %collective-permute-done.9.refs_2_), channel_id=1, source_target_pairs={{0,480},{32,0},{64,32},{96,64},{128,96},{160,128},{192,160},{224,1... | collective-permute-start | bytes 1536008 | tf_op jit(solution)/shard_map/ppermute | solution.py:253
  90.3 9.2 %collective-permute-done.2.refs_3_ = bf16[1000,256]{1,0:T(8,128)(2,1)S(1)} collective-permute-done((bf16[1000,256]{1,0:T(8,128)(2,1)S(1)}, bf16[1000,256]{1,0:T(8,128)(2,1)S(1)}, u32[]{:S(2)}, u32[]{:S(2)}) %collective-permute-start.2) | collective-permute-done | bytes 512032 | tf_op jit(solution)/shard_map/ppermute | solution.py:251
  99.5 1.9 collective-permute-start.3
  101.4 0.0 collective-permute-done.10.refs_4_
  101.4 4.6 %collective-permute-start.11 = (bf16[1000,256]{1,0:T(8,128)(2,1)S(1)}, bf16[1000,256]{1,0:T(8,128)(2,1)S(1)}, u32[]{:S(2)}, u32[]{:S(2)}) collective-permute-start(bf16[1000,256]{1,0:T(8,128)(2,1)S(1)} %collective-permute-done.10.refs_4_), channel_id=1, source_target_pairs={{0,480},{32,0},{64,32},{96,64},{128,96},{160,128},{192,160},{224,1... | collective-permute-start | bytes 1536008 | tf_op jit(solution)/shard_map/ppermute | solution.py:253
  106.0 8.4 %collective-permute-done.3.refs_5_ = bf16[1000,256]{1,0:T(8,128)(2,1)S(1)} collective-permute-done((bf16[1000,256]{1,0:T(8,128)(2,1)S(1)}, bf16[1000,256]{1,0:T(8,128)(2,1)S(1)}, u32[]{:S(2)}, u32[]{:S(2)}) %collective-permute-start.3) | collective-permute-done | bytes 512032 | tf_op jit(solution)/shard_map/ppermute | solution.py:251
  114.4 1.9 collective-permute-start.4
  116.3 0.0 collective-permute-done.11.refs_6_
  116.3 4.6 %collective-permute-start.12 = (bf16[1000,256]{1,0:T(8,128)(2,1)S(1)}, bf16[1000,256]{1,0:T(8,128)(2,1)S(1)}, u32[]{:S(2)}, u32[]{:S(2)}) collective-permute-start(bf16[1000,256]{1,0:T(8,128)(2,1)S(1)} %collective-permute-done.11.refs_6_), channel_id=1, source_target_pairs={{0,480},{32,0},{64,32},{96,64},{128,96},{160,128},{192,160},{224,1... | collective-permute-start | bytes 1536008 | tf_op jit(solution)/shard_map/ppermute | solution.py:253
  120.9 7.5 %collective-permute-done.4.refs_0_ = bf16[1000,256]{1,0:T(8,128)(2,1)S(1)} collective-permute-done((bf16[1000,256]{1,0:T(8,128)(2,1)S(1)}, bf16[1000,256]{1,0:T(8,128)(2,1)S(1)}, u32[]{:S(2)}, u32[]{:S(2)}) %collective-permute-start.4) | collective-permute-done | bytes 512032 | tf_op jit(solution)/shard_map/ppermute | solution.py:251
  128.4 1.9 collective-permute-start.5
  130.3 0.0 collective-permute-done.12.refs_1_
  130.3 4.6 %collective-permute-start.13 = (bf16[1000,256]{1,0:T(8,128)(2,1)S(1)}, bf16[1000,256]{1,0:T(8,128)(2,1)S(1)}, u32[]{:S(2)}, u32[]{:S(2)}) collective-permute-start(bf16[1000,256]{1,0:T(8,128)(2,1)S(1)} %collective-permute-done.12.refs_1_), channel_id=1, source_target_pairs={{0,480},{32,0},{64,32},{96,64},{128,96},{160,128},{192,160},{224,1... | collective-permute-start | bytes 1536008 | tf_op jit(solution)/shard_map/ppermute | solution.py:253
  134.9 6.6 %collective-permute-done.5.refs_2_ = bf16[1000,256]{1,0:T(8,128)(2,1)S(1)} collective-permute-done((bf16[1000,256]{1,0:T(8,128)(2,1)S(1)}, bf16[1000,256]{1,0:T(8,128)(2,1)S(1)}, u32[]{:S(2)}, u32[]{:S(2)}) %collective-permute-start.5) | collective-permute-done | bytes 512032 | tf_op jit(solution)/shard_map/ppermute | solution.py:251
  141.5 1.9 collective-permute-start.6
  143.4 0.0 collective-permute-done.13.refs_3_
  143.4 4.6 %collective-permute-start.14 = (bf16[1000,256]{1,0:T(8,128)(2,1)S(1)}, bf16[1000,256]{1,0:T(8,128)(2,1)S(1)}, u32[]{:S(2)}, u32[]{:S(2)}) collective-permute-start(bf16[1000,256]{1,0:T(8,128)(2,1)S(1)} %collective-permute-done.13.refs_3_), channel_id=1, source_target_pairs={{0,480},{32,0},{64,32},{96,64},{128,96},{160,128},{192,160},{224,1... | collective-permute-start | bytes 1536008 | tf_op jit(solution)/shard_map/ppermute | solution.py:253
  148.0 5.8 %collective-permute-done.6.refs_4_ = bf16[1000,256]{1,0:T(8,128)(2,1)S(1)} collective-permute-done((bf16[1000,256]{1,0:T(8,128)(2,1)S(1)}, bf16[1000,256]{1,0:T(8,128)(2,1)S(1)}, u32[]{:S(2)}, u32[]{:S(2)}) %collective-permute-start.6) | collective-permute-done | bytes 512032 | tf_op jit(solution)/shard_map/ppermute | solution.py:251
  153.8 1.9 collective-permute-start.7
  155.7 0.0 collective-permute-done.14.refs_5_
  155.7 4.6 %collective-permute-start.15 = (bf16[1000,256]{1,0:T(8,128)(2,1)S(1)}, bf16[1000,256]{1,0:T(8,128)(2,1)S(1)}, u32[]{:S(2)}, u32[]{:S(2)}) collective-permute-start(bf16[1000,256]{1,0:T(8,128)(2,1)S(1)} %collective-permute-done.14.refs_5_), channel_id=1, source_target_pairs={{0,480},{32,0},{64,32},{96,64},{128,96},{160,128},{192,160},{224,1... | collective-permute-start | bytes 1536008 | tf_op jit(solution)/shard_map/ppermute | solution.py:253
  160.3 4.9 %collective-permute-done.7.refs_6_ = bf16[1000,256]{1,0:T(8,128)(2,1)S(1)} collective-permute-done((bf16[1000,256]{1,0:T(8,128)(2,1)S(1)}, bf16[1000,256]{1,0:T(8,128)(2,1)S(1)}, u32[]{:S(2)}, u32[]{:S(2)}) %collective-permute-start.7) | collective-permute-done | bytes 512032 | tf_op jit(solution)/shard_map/ppermute | solution.py:251
  165.3 1.9 collective-permute-start.8
  167.2 0.0 collective-permute-done.two_ref.gain_two_ref
  167.2 6.4 %norm.1 = (bf16[16,896,256]{2,1,0:T(8,128)(2,1)S(1)}, f32[2,16,16,128]{3,2,1,0:T(8,128)S(1)}) custom-call(bf16[16,912,128]{2,1,0:T(8,128)(2,1)S(1)} %all_to_all.16.one_ref.gain_one_ref, bf16[16,912,128]{2,1,0:T(8,128)(2,1)S(1)} %collective-permute-done.two_ref.gain_two_ref, bf16[16,912,128]{2,1,0:T(8,128)(2,1)S(1)} %all_to_all.16.one_ref.gain_one_ref, ...), custom_call_target="tpu_custom_call" | custom-call | flops 22413312 | bytes 14942208 | tf_op jit(solution)/shard_map/norm/pallas_call | solution.py:99
  173.6 3.9 %scores.2.refs_8_ = f32[1000,896]{1,0:T(8,128)S(1)} custom-call(bf16[16,896,256]{2,1,0:T(8,128)(2,1)S(1)} %get-tuple-element.8.n_ref, bf16[1000,256]{1,0:T(8,128)(2,1)S(1)} %bitcast.12, bf16[1000,256]{1,0:T(8,128)(2,1)S(1)} %collective-permute-done.1.refs_1_, bf16[1000,256]{1,0:T(8,128)(2,1)S(1)} %collective-permute-done.9.refs_2_, ...), custom_call_target="tpu_custom_call" | custom-call | flops 3211264000 | bytes 7168000 | tf_op jit(solution)/shard_map/scores/pallas_call | solution.py:145
  177.5 0.0 copy-start.1
  177.5 0.0 collective-permute-done.15.refs_7_
  177.5 4.5 %scores.3.acc_ref = f32[1000,896]{1,0:T(8,128)S(1)} custom-call(bf16[16,896,256]{2,1,0:T(8,128)(2,1)S(1)} %get-tuple-element.8.n_ref, bf16[1000,256]{1,0:T(8,128)(2,1)S(1)} %collective-permute-done.4.refs_0_, bf16[1000,256]{1,0:T(8,128)(2,1)S(1)} %collective-permute-done.12.refs_1_, ...), custom_call_target="tpu_custom_call", output_to_operand_aliasing={{}: (9, {})} | custom-call | flops 3670016000 | bytes 7168000 | tf_op jit(solution)/shard_map/scores/pallas_call | solution.py:145
  182.0 0.0 collective-permute-done.8.w_ref
  182.0 0.0 copy-done.1
  182.1 1.9 stats.1
  183.9 0.8 broadcast_in_dim.23
  184.7 9.3 %all-to-all-start.1 = ((f32[32,4,896]{2,1,0:T(4,128)}), f32[32,4,896]{2,1,0:T(4,128)S(1)}, u32[]{:S(2)}, u32[]{:S(2)}) async-start(f32[32,4,896]{2,1,0:T(4,128)} %broadcast_in_dim.23), calls=%async_computation.1 | async-start | bytes 917504 | tf_op jit(solution)/shard_map/all_to_all | solution.py:275
  194.1 0.1 convert_element_type.6.seq_ref
  194.2 0.1 squeeze.10.live_ref
  194.3 10.7 %all-to-all-done.1.x_ref = f32[32,4,896]{2,1,0:T(4,128)S(1)} async-done(((f32[32,4,896]{2,1,0:T(4,128)}), f32[32,4,896]{2,1,0:T(4,128)S(1)}, u32[]{:S(2)}, u32[]{:S(2)}) %all-to-all-start.1) | async-done | bytes 458784 | tf_op jit(solution)/shard_map/all_to_all | solution.py:275
  205.1 1.6 combine.1
  206.6 18.6 %all_to_all.17 = f32[16,1,128]{2,1,0:T(1,128)S(1)} all-to-all(f32[16,1,128]{2,1,0:T(1,128)S(1)} %broadcast_in_dim.24), channel_id=1, replica_groups=mesh['dp'=16,'tensor'=32] {'dp'}, dimensions={0} | all-to-all | bytes 16384 | tf_op jit(solution)/shard_map/all_to_all | solution.py:279
  225.2 0.6 maximum_divide_fusion
  (6 shorter events, 0.1 us)
Async XLA Ops:
  3.6 56.5 %copy-start = (bf16[256,1000]{0,1:T(8,128)(2,1)S(1)}, bf16[256,1000]{0,1:T(8,128)(2,1)}, u32[]{:S(2)}) copy-start(bf16[256,1000]{0,1:T(8,128)(2,1)} %param.8) | copy-start | bytes 1536004
  54.2 113.0 %collective-permute-start = (bf16[16,912,128]{2,1,0:T(8,128)(2,1)S(1)}, bf16[16,912,128]{2,1,0:T(8,128)(2,1)S(1)}, u32[]{:S(2)}, u32[]{:S(2)}) collective-permute-start(bf16[16,912,128]{2,1,0:T(8,128)(2,1)S(1)} %all_to_all.16.one_ref.gain_one_ref), channel_id=1, source_target_pairs={{0,1},{1,0},{2,3},{3,2},{4,5},{5,4},{6,7},{7,6},{8,9},{9,8},{10,11... | collective-permute-start | bytes 11206664 | tf_op jit(solution)/shard_map/ppermute | solution.py:262
  60.1 23.7 %collective-permute-start.1 = (bf16[1000,256]{1,0:T(8,128)(2,1)S(1)}, bf16[1000,256]{1,0:T(8,128)(2,1)S(1)}, u32[]{:S(2)}, u32[]{:S(2)}) collective-permute-start(bf16[1000,256]{1,0:T(8,128)(2,1)S(1)} %bitcast.10), channel_id=1, source_target_pairs={{0,32},{32,64},{64,96},{96,128},{128,160},{160,192},{192,224},{224... | collective-permute-start | bytes 1536008 | tf_op jit(solution)/shard_map/ppermute | solution.py:251
  64.2 21.5 %collective-permute-start.9 = (bf16[1000,256]{1,0:T(8,128)(2,1)S(1)}, bf16[1000,256]{1,0:T(8,128)(2,1)S(1)}, u32[]{:S(2)}, u32[]{:S(2)}) collective-permute-start(bf16[1000,256]{1,0:T(8,128)(2,1)S(1)} %bitcast.11), channel_id=1, source_target_pairs={{0,480},{32,0},{64,32},{96,64},{128,96},{160,128},{192,160},{224,1... | collective-permute-start | bytes 1536008 | tf_op jit(solution)/shard_map/ppermute | solution.py:253
  83.8 15.7 %collective-permute-start.2 = (bf16[1000,256]{1,0:T(8,128)(2,1)S(1)}, bf16[1000,256]{1,0:T(8,128)(2,1)S(1)}, u32[]{:S(2)}, u32[]{:S(2)}) collective-permute-start(bf16[1000,256]{1,0:T(8,128)(2,1)S(1)} %collective-permute-done.1.refs_1_), channel_id=1, source_target_pairs={{0,32},{32,64},{64,96},{96,128},{128,160},{160,192},{192,224},{224... | collective-permute-start | bytes 1536008 | tf_op jit(solution)/shard_map/ppermute | solution.py:251
  85.7 15.7 %collective-permute-start.10 = (bf16[1000,256]{1,0:T(8,128)(2,1)S(1)}, bf16[1000,256]{1,0:T(8,128)(2,1)S(1)}, u32[]{:S(2)}, u32[]{:S(2)}) collective-permute-start(bf16[1000,256]{1,0:T(8,128)(2,1)S(1)} %collective-permute-done.9.refs_2_), channel_id=1, source_target_pairs={{0,480},{32,0},{64,32},{96,64},{128,96},{160,128},{192,160},{224,1... | collective-permute-start | bytes 1536008 | tf_op jit(solution)/shard_map/ppermute | solution.py:253
  99.5 14.9 %collective-permute-start.3 = (bf16[1000,256]{1,0:T(8,128)(2,1)S(1)}, bf16[1000,256]{1,0:T(8,128)(2,1)S(1)}, u32[]{:S(2)}, u32[]{:S(2)}) collective-permute-start(bf16[1000,256]{1,0:T(8,128)(2,1)S(1)} %collective-permute-done.2.refs_3_), channel_id=1, source_target_pairs={{0,32},{32,64},{64,96},{96,128},{128,160},{160,192},{192,224},{224... | collective-permute-start | bytes 1536008 | tf_op jit(solution)/shard_map/ppermute | solution.py:251
  101.4 14.9 %collective-permute-start.11 = (bf16[1000,256]{1,0:T(8,128)(2,1)S(1)}, bf16[1000,256]{1,0:T(8,128)(2,1)S(1)}, u32[]{:S(2)}, u32[]{:S(2)}) collective-permute-start(bf16[1000,256]{1,0:T(8,128)(2,1)S(1)} %collective-permute-done.10.refs_4_), channel_id=1, source_target_pairs={{0,480},{32,0},{64,32},{96,64},{128,96},{160,128},{192,160},{224,1... | collective-permute-start | bytes 1536008 | tf_op jit(solution)/shard_map/ppermute | solution.py:253
  114.4 14.0 %collective-permute-start.4 = (bf16[1000,256]{1,0:T(8,128)(2,1)S(1)}, bf16[1000,256]{1,0:T(8,128)(2,1)S(1)}, u32[]{:S(2)}, u32[]{:S(2)}) collective-permute-start(bf16[1000,256]{1,0:T(8,128)(2,1)S(1)} %collective-permute-done.3.refs_5_), channel_id=1, source_target_pairs={{0,32},{32,64},{64,96},{96,128},{128,160},{160,192},{192,224},{224... | collective-permute-start | bytes 1536008 | tf_op jit(solution)/shard_map/ppermute | solution.py:251
  116.3 14.0 %collective-permute-start.12 = (bf16[1000,256]{1,0:T(8,128)(2,1)S(1)}, bf16[1000,256]{1,0:T(8,128)(2,1)S(1)}, u32[]{:S(2)}, u32[]{:S(2)}) collective-permute-start(bf16[1000,256]{1,0:T(8,128)(2,1)S(1)} %collective-permute-done.11.refs_6_), channel_id=1, source_target_pairs={{0,480},{32,0},{64,32},{96,64},{128,96},{160,128},{192,160},{224,1... | collective-permute-start | bytes 1536008 | tf_op jit(solution)/shard_map/ppermute | solution.py:253
  128.4 13.2 %collective-permute-start.5 = (bf16[1000,256]{1,0:T(8,128)(2,1)S(1)}, bf16[1000,256]{1,0:T(8,128)(2,1)S(1)}, u32[]{:S(2)}, u32[]{:S(2)}) collective-permute-start(bf16[1000,256]{1,0:T(8,128)(2,1)S(1)} %collective-permute-done.4.refs_0_), channel_id=1, source_target_pairs={{0,32},{32,64},{64,96},{96,128},{128,160},{160,192},{192,224},{224... | collective-permute-start | bytes 1536008 | tf_op jit(solution)/shard_map/ppermute | solution.py:251
  130.3 13.1 %collective-permute-start.13 = (bf16[1000,256]{1,0:T(8,128)(2,1)S(1)}, bf16[1000,256]{1,0:T(8,128)(2,1)S(1)}, u32[]{:S(2)}, u32[]{:S(2)}) collective-permute-start(bf16[1000,256]{1,0:T(8,128)(2,1)S(1)} %collective-permute-done.12.refs_1_), channel_id=1, source_target_pairs={{0,480},{32,0},{64,32},{96,64},{128,96},{160,128},{192,160},{224,1... | collective-permute-start | bytes 1536008 | tf_op jit(solution)/shard_map/ppermute | solution.py:253
  141.5 12.3 %collective-permute-start.6 = (bf16[1000,256]{1,0:T(8,128)(2,1)S(1)}, bf16[1000,256]{1,0:T(8,128)(2,1)S(1)}, u32[]{:S(2)}, u32[]{:S(2)}) collective-permute-start(bf16[1000,256]{1,0:T(8,128)(2,1)S(1)} %collective-permute-done.5.refs_2_), channel_id=1, source_target_pairs={{0,32},{32,64},{64,96},{96,128},{128,160},{160,192},{192,224},{224... | collective-permute-start | bytes 1536008 | tf_op jit(solution)/shard_map/ppermute | solution.py:251
  143.4 12.3 %collective-permute-start.14 = (bf16[1000,256]{1,0:T(8,128)(2,1)S(1)}, bf16[1000,256]{1,0:T(8,128)(2,1)S(1)}, u32[]{:S(2)}, u32[]{:S(2)}) collective-permute-start(bf16[1000,256]{1,0:T(8,128)(2,1)S(1)} %collective-permute-done.13.refs_3_), channel_id=1, source_target_pairs={{0,480},{32,0},{64,32},{96,64},{128,96},{160,128},{192,160},{224,1... | collective-permute-start | bytes 1536008 | tf_op jit(solution)/shard_map/ppermute | solution.py:253
  153.8 11.4 %collective-permute-start.7 = (bf16[1000,256]{1,0:T(8,128)(2,1)S(1)}, bf16[1000,256]{1,0:T(8,128)(2,1)S(1)}, u32[]{:S(2)}, u32[]{:S(2)}) collective-permute-start(bf16[1000,256]{1,0:T(8,128)(2,1)S(1)} %collective-permute-done.6.refs_4_), channel_id=1, source_target_pairs={{0,32},{32,64},{64,96},{96,128},{128,160},{160,192},{192,224},{224... | collective-permute-start | bytes 1536008 | tf_op jit(solution)/shard_map/ppermute | solution.py:251
  155.7 21.8 %collective-permute-start.15 = (bf16[1000,256]{1,0:T(8,128)(2,1)S(1)}, bf16[1000,256]{1,0:T(8,128)(2,1)S(1)}, u32[]{:S(2)}, u32[]{:S(2)}) collective-permute-start(bf16[1000,256]{1,0:T(8,128)(2,1)S(1)} %collective-permute-done.14.refs_5_), channel_id=1, source_target_pairs={{0,480},{32,0},{64,32},{96,64},{128,96},{160,128},{192,160},{224,1... | collective-permute-start | bytes 1536008 | tf_op jit(solution)/shard_map/ppermute | solution.py:253
  165.3 16.8 %collective-permute-start.8 = (bf16[1000,256]{1,0:T(8,128)(2,1)S(1)}, bf16[1000,256]{1,0:T(8,128)(2,1)S(1)}, u32[]{:S(2)}, u32[]{:S(2)}) collective-permute-start(bf16[1000,256]{1,0:T(8,128)(2,1)S(1)} %collective-permute-done.7.refs_6_), channel_id=1, source_target_pairs={{0,32},{32,64},{64,96},{96,128},{128,160},{160,192},{192,224},{224... | collective-permute-start | bytes 1536008 | tf_op jit(solution)/shard_map/ppermute | solution.py:251
  177.5 4.5 %copy-start.1 = (s32[896]{0:T(1024)S(1)}, s32[896]{0:T(1024)}, u32[]{:S(2)}) copy-start(s32[896]{0:T(1024)} %ids_ref.1) | copy-start | bytes 10756
  184.7 20.3 %all-to-all-start.1 = ((f32[32,4,896]{2,1,0:T(4,128)}), f32[32,4,896]{2,1,0:T(4,128)S(1)}, u32[]{:S(2)}, u32[]{:S(2)}) async-start(f32[32,4,896]{2,1,0:T(4,128)} %broadcast_in_dim.23), calls=%async_computation.1 | async-start | bytes 917504 | tf_op jit(solution)/shard_map/all_to_all | solution.py:275

commit v4 on v3

--- a/solution.py
+++ b/solution.py
@@ -65,53 +65,77 @@
         ],
         compiler_params=room(4),
         name="fan",
-    )(*(pltpu.with_memory_space_constraint(x, pltpu.HBM) for x in (hidden, gain[None], seq_ids[None], live[None])))
-
-
-def norm_kernel(one_ref, two_ref, gain_one_ref, gain_two_ref, out_ref, flag_ref):
-    chips, step, lanes = one_ref.shape
+    )(
+        *(
+            pltpu.with_memory_space_constraint(x, pltpu.HBM)
+            for x in (hidden, gain[None], seq_ids[None], live[None])
+        )
+    )
+
+
+def norm_kernel(one_ref, two_ref, out_ref, flag_ref, buf_ref, sems):
+    _, chips, rows, lanes = buf_ref.shape
+    tokens, step = rows - EXTRA, 128
     core = lax.axis_index("tensor") % 2
 
-    @pl.when(pl.program_id(0) == 0)
-    def _():
-        flag_ref[core] = gain_one_ref[...].astype(jnp.float32)
-        flag_ref[1 - core] = gain_two_ref[...].astype(jnp.float32)
-
-    square = jnp.zeros((step, lanes), jnp.float32)
-    for ref in (one_ref, two_ref):
-        for t in range(chips):
-            v = ref[t].astype(jnp.float32)
-            square = square + v * v
-    mean = jnp.sum(square, axis=-1, keepdims=True) / (2 * chips * lanes)
-    scale = lax.rsqrt(mean + 1e-05)
-    for ref, gain_ref, half in ((one_ref, gain_one_ref, core), (two_ref, gain_two_ref, 1 - core)):
-        to = pl.ds(pl.multiple_of(half * lanes, lanes), lanes)
-        for t in range(chips):
-            gain = gain_ref[t].astype(jnp.float32)[0:1, :]
-            out_ref[t, :, to] = (ref[t].astype(jnp.float32) * scale * gain).astype(jnp.bfloat16)
+    def load(i, first, size):
+        span = pl.ds(first, size)
+        return [
+            pltpu.make_async_copy(ref.at[:, span, :], buf_ref.at[r, :, span, :], sems.at[r, i])
+            for r, ref in enumerate((one_ref, two_ref))
+        ]
+
+    count = tokens // step
+    under = load(count, tokens, EXTRA)
+    for copy in sum((load(i, i * step, step) for i in range(count)), under):
+        copy.start()
+    for copy in under:
+        copy.wait()
+    for r, half in enumerate((core, 1 - core)):
+        flag_ref[half] = buf_ref[r, :, tokens:rows, :].astype(jnp.float32)
+
+    def block(i, carry):
+        first = pl.multiple_of(i * step, step)
+        for copy in load(i, first, step):
+            copy.wait()
+        at = pl.ds(first, step)
+        square = jnp.zeros((step, lanes), jnp.float32)
+        for r in range(2):
+            for t in range(chips):
+                v = buf_ref[r, t, at, :].astype(jnp.float32)
+                square = square + v * v
+        mean = jnp.sum(square, axis=-1, keepdims=True) / (2 * chips * lanes)
+        scale = lax.rsqrt(mean + 1e-05)
+        for r, half in enumerate((core, 1 - core)):
+            to = pl.ds(pl.multiple_of(half * lanes, lanes), lanes)
+            for t in range(chips):
+                v = buf_ref[r, t, at, :].astype(jnp.float32)
+                gain = flag_ref[half, t, 0:1, :]
+                out_ref[t, at, to] = (v * scale * gain).astype(jnp.bfloat16)
+        return carry
+
+    lax.fori_loop(0, count, block, 0)
 
 
 def normalise(one, two):
     chips, rows, lanes = one.shape
-    tokens, step = rows - EXTRA, 128
-    part = pl.BlockSpec((chips, step, lanes), lambda i: (0, i, 0))
-    gain = pl.BlockSpec((chips, EXTRA, lanes), lambda i: (0, tokens // EXTRA, 0))
+    tokens = rows - EXTRA
     return pl.pallas_call(
         norm_kernel,
-        grid=(tokens // step,),
         out_shape=(
             jax.ShapeDtypeStruct((chips, tokens, 2 * lanes), jnp.bfloat16),
             jax.ShapeDtypeStruct((2, chips, EXTRA, lanes), jnp.float32),
         ),
-        in_specs=[part, part, gain, gain],
-        out_specs=(
-            pl.BlockSpec((chips, step, 2 * lanes), lambda i: (0, i, 0)),
-            pl.BlockSpec((2, chips, EXTRA, lanes), lambda i: (0, 0, 0, 0)),
-        ),
-        compiler_params=room(8),
+        in_specs=[pl.BlockSpec(memory_space=pl.ANY)] * 2,
+        out_specs=(VM, VM),
+        scratch_shapes=[
+            pltpu.VMEM((2, chips, rows, lanes), jnp.bfloat16),
+            pltpu.SemaphoreType.DMA((2, tokens // 128 + 1)),
+        ],
+        compiler_params=room(12),
         cost_estimate=cost(12 * one.size, 8 * one.size),
         name="norm",
-    )(one, two, one, two)
+    )(one, two)
 
 
 def product(w, x):
@@ -266,8 +290,8 @@
         chunks += [a, b]
     last, _ = turn(a, b, ring // 2)
     aheads = [0] + [s if i else -s for s in range(1, ring // 2 + 1) for i in range(2)]
-    acc = accumulate(aheads[0:7], normed, chunks[0:7])
-    acc = accumulate(aheads[7:15], normed, chunks[7:15], acc)
+    acc = accumulate(aheads[0:5], normed, chunks[0:5])
+    acc = accumulate(aheads[5:15], normed, chunks[5:15], acc)
     flags = extra[:, :, 1:3, :share].transpose(2, 1, 0, 3).reshape(2, 1, tokens)
     seq, alive = flags[0].astype(jnp.int32), flags[1]
     stats = statistics(ring // 2, normed, last, acc, targets)

time: 227 us -> 225 us (level)
  transfers between devices with their start and end apart: 17 -> 17, of which waited for: 8 -> 8; matrix products, arithmetic and copies ran while one was open for 0% -> 0% of each run, Pallas kernels for 7% -> 6%
where the time goes in v4:
time: 225 us; the launch traced here: 224 us
  starting transfers between devices  69.6 us (31%)
  blocking collectives  69.1 us (31%)
  waiting for transfers between devices  63.3 us (28%)
  Pallas kernels  19.3 us (9%)
    ppermute x8, waiting for transfers between devices, turn(): a = lax.ppermute(a, 'dp', forth)  52.5 us
    all_to_all x1, blocking collectives, body(): one = lax.all_to_all(sent, 'tensor', 0, 0, axis_index_groups=teams)  50.6 us
    ppermute x7, starting transfers between devices, turn(): b = lax.ppermute(b, 'dp', back)  36.9 us
    all_to_all x1, blocking collectives, body(): lax.all_to_all(jnp.broadcast_to(sums, (ring, 2 * SEQS)), 'dp', 0, 0)  18.6 us
    ppermute x8, starting transfers between devices, turn(): a = lax.ppermute(a, 'dp', forth)  17.4 us
    all_to_all x1, waiting for transfers between devices, body(): lax.all_to_all(jnp.broadcast_to(stats[None], (shards, *stats.shape)), 'te...  10.7 us
    all_to_all x1, starting transfers between devices, body(): lax.all_to_all(jnp.broadcast_to(stats[None], (shards, *stats.shape)), 'te...  9.28 us
    pallas_call x2, Pallas kernels, accumulate(): pl.pallas_call(functools.partial(mm_kernel, tuple(aheads)), out_shape=jax...  8.41 us
  transfers between devices with their start and end apart: 17, of which 8 were waited for; matrix products, arithmetic and copies ran while one was open for 0% of the time, Pallas kernels for 6%

profile of v4, /device:TPU:1, one launch (start us, length us, event | category | flops | bytes accessed | tf_op | source)
XLA Modules:
  0.0 224.0 jit_solution(6761079171769960339)
XLA Ops:
  0.6 2.9 %fan.1 = bf16[16,912,128]{2,1,0:T(8,128)(2,1)} custom-call(bf16[896,128]{1,0:T(8,128)(2,1)} %hid_ref.1, bf16[1,128]{1,0:T(2,128)(2,1)} %bitcast.15, s32[1,28]{1,0:T(1,128)} %bitcast.16, s32[1,28]{1,0:T(1,128)} %bitcast.17), custom_call_target="tpu_custom_call" | custom-call | tf_op jit(solution)/shard_map/fan/pallas_call | solution.py:53
  3.6 0.0 copy-start
  3.6 50.6 %all_to_all.16.one_ref = bf16[16,912,128]{2,1,0:T(8,128)(2,1)S(1)} all-to-all(bf16[16,912,128]{2,1,0:T(8,128)(2,1)} %fan.1), channel_id=1, replica_groups={{0,2,4,6,8,10,12,14,16,18,20,22,24,26,28,30},{1,3,5,7,9,11,13,15,17,19,..., dimensions={0} | all-to-all | bytes 7471104 | tf_op jit(solution)/shard_map/all_to_all | solution.py:285
  54.2 5.9 %collective-permute-start = (bf16[16,912,128]{2,1,0:T(8,128)(2,1)S(1)}, bf16[16,912,128]{2,1,0:T(8,128)(2,1)S(1)}, u32[]{:S(2)}, u32[]{:S(2)}) collective-permute-start(bf16[16,912,128]{2,1,0:T(8,128)(2,1)S(1)} %all_to_all.16.one_ref), channel_id=1, source_target_pairs={{0,1},{1,0},{2,3},{3,2},{4,5},{5,4},{6,7},{7,6},{8,9},{9,8},{10,11... | collective-permute-start | bytes 11206664 | tf_op jit(solution)/shard_map/ppermute | solution.py:286
  60.1 0.0 copy-done
  60.1 4.1 %collective-permute-start.1 = (bf16[1000,256]{1,0:T(8,128)(2,1)S(1)}, bf16[1000,256]{1,0:T(8,128)(2,1)S(1)}, u32[]{:S(2)}, u32[]{:S(2)}) collective-permute-start(bf16[1000,256]{1,0:T(8,128)(2,1)S(1)} %bitcast.10), channel_id=1, source_target_pairs={{0,32},{32,64},{64,96},{96,128},{128,160},{160,192},{192,224},{224... | collective-permute-start | bytes 1536008 | tf_op jit(solution)/shard_map/ppermute | solution.py:275
  64.2 9.5 %collective-permute-start.9 = (bf16[1000,256]{1,0:T(8,128)(2,1)S(1)}, bf16[1000,256]{1,0:T(8,128)(2,1)S(1)}, u32[]{:S(2)}, u32[]{:S(2)}) collective-permute-start(bf16[1000,256]{1,0:T(8,128)(2,1)S(1)} %bitcast.11), channel_id=1, source_target_pairs={{0,480},{32,0},{64,32},{96,64},{128,96},{160,128},{192,160},{224,1... | collective-permute-start | bytes 1536008 | tf_op jit(solution)/shard_map/ppermute | solution.py:277
  73.7 10.1 %collective-permute-done.1.refs_1_ = bf16[1000,256]{1,0:T(8,128)(2,1)S(1)} collective-permute-done((bf16[1000,256]{1,0:T(8,128)(2,1)S(1)}, bf16[1000,256]{1,0:T(8,128)(2,1)S(1)}, u32[]{:S(2)}, u32[]{:S(2)}) %collective-permute-start.1) | collective-permute-done | bytes 512032 | tf_op jit(solution)/shard_map/ppermute | solution.py:275
  83.8 1.9 collective-permute-start.2
  85.7 0.0 collective-permute-done.9.refs_2_
  85.7 4.6 %collective-permute-start.10 = (bf16[1000,256]{1,0:T(8,128)(2,1)S(1)}, bf16[1000,256]{1,0:T(8,128)(2,1)S(1)}, u32[]{:S(2)}, u32[]{:S(2)}) collective-permute-start(bf16[1000,256]{1,0:T(8,128)(2,1)S(1)} %collective-permute-done.9.refs_2_), channel_id=1, source_target_pairs={{0,480},{32,0},{64,32},{96,64},{128,96},{160,128},{192,160},{224,1... | collective-permute-start | bytes 1536008 | tf_op jit(solution)/shard_map/ppermute | solution.py:277
  90.3 9.2 %collective-permute-done.2.refs_3_ = bf16[1000,256]{1,0:T(8,128)(2,1)S(1)} collective-permute-done((bf16[1000,256]{1,0:T(8,128)(2,1)S(1)}, bf16[1000,256]{1,0:T(8,128)(2,1)S(1)}, u32[]{:S(2)}, u32[]{:S(2)}) %collective-permute-start.2) | collective-permute-done | bytes 512032 | tf_op jit(solution)/shard_map/ppermute | solution.py:275
  99.5 1.9 collective-permute-start.3
  101.4 0.0 collective-permute-done.10.refs_4_
  101.4 4.6 %collective-permute-start.11 = (bf16[1000,256]{1,0:T(8,128)(2,1)S(1)}, bf16[1000,256]{1,0:T(8,128)(2,1)S(1)}, u32[]{:S(2)}, u32[]{:S(2)}) collective-permute-start(bf16[1000,256]{1,0:T(8,128)(2,1)S(1)} %collective-permute-done.10.refs_4_), channel_id=1, source_target_pairs={{0,480},{32,0},{64,32},{96,64},{128,96},{160,128},{192,160},{224,1... | collective-permute-start | bytes 1536008 | tf_op jit(solution)/shard_map/ppermute | solution.py:277
  106.0 8.4 %collective-permute-done.3.refs_0_ = bf16[1000,256]{1,0:T(8,128)(2,1)S(1)} collective-permute-done((bf16[1000,256]{1,0:T(8,128)(2,1)S(1)}, bf16[1000,256]{1,0:T(8,128)(2,1)S(1)}, u32[]{:S(2)}, u32[]{:S(2)}) %collective-permute-start.3) | collective-permute-done | bytes 512032 | tf_op jit(solution)/shard_map/ppermute | solution.py:275
  114.4 1.9 collective-permute-start.4
  116.3 0.0 collective-permute-done.11.refs_1_
  116.3 4.6 %collective-permute-start.12 = (bf16[1000,256]{1,0:T(8,128)(2,1)S(1)}, bf16[1000,256]{1,0:T(8,128)(2,1)S(1)}, u32[]{:S(2)}, u32[]{:S(2)}) collective-permute-start(bf16[1000,256]{1,0:T(8,128)(2,1)S(1)} %collective-permute-done.11.refs_1_), channel_id=1, source_target_pairs={{0,480},{32,0},{64,32},{96,64},{128,96},{160,128},{192,160},{224,1... | collective-permute-start | bytes 1536008 | tf_op jit(solution)/shard_map/ppermute | solution.py:277
  120.9 7.5 %collective-permute-done.4.refs_2_ = bf16[1000,256]{1,0:T(8,128)(2,1)S(1)} collective-permute-done((bf16[1000,256]{1,0:T(8,128)(2,1)S(1)}, bf16[1000,256]{1,0:T(8,128)(2,1)S(1)}, u32[]{:S(2)}, u32[]{:S(2)}) %collective-permute-start.4) | collective-permute-done | bytes 512032 | tf_op jit(solution)/shard_map/ppermute | solution.py:275
  128.4 1.9 collective-permute-start.5
  130.3 0.0 collective-permute-done.12.refs_3_
  130.3 4.6 %collective-permute-start.13 = (bf16[1000,256]{1,0:T(8,128)(2,1)S(1)}, bf16[1000,256]{1,0:T(8,128)(2,1)S(1)}, u32[]{:S(2)}, u32[]{:S(2)}) collective-permute-start(bf16[1000,256]{1,0:T(8,128)(2,1)S(1)} %collective-permute-done.12.refs_3_), channel_id=1, source_target_pairs={{0,480},{32,0},{64,32},{96,64},{128,96},{160,128},{192,160},{224,1... | collective-permute-start | bytes 1536008 | tf_op jit(solution)/shard_map/ppermute | solution.py:277
  134.9 6.6 %collective-permute-done.5.refs_4_ = bf16[1000,256]{1,0:T(8,128)(2,1)S(1)} collective-permute-done((bf16[1000,256]{1,0:T(8,128)(2,1)S(1)}, bf16[1000,256]{1,0:T(8,128)(2,1)S(1)}, u32[]{:S(2)}, u32[]{:S(2)}) %collective-permute-start.5) | collective-permute-done | bytes 512032 | tf_op jit(solution)/shard_map/ppermute | solution.py:275
  141.5 1.9 collective-permute-start.6
  143.4 0.0 collective-permute-done.13.refs_5_
  143.4 4.6 %collective-permute-start.14 = (bf16[1000,256]{1,0:T(8,128)(2,1)S(1)}, bf16[1000,256]{1,0:T(8,128)(2,1)S(1)}, u32[]{:S(2)}, u32[]{:S(2)}) collective-permute-start(bf16[1000,256]{1,0:T(8,128)(2,1)S(1)} %collective-permute-done.13.refs_5_), channel_id=1, source_target_pairs={{0,480},{32,0},{64,32},{96,64},{128,96},{160,128},{192,160},{224,1... | collective-permute-start | bytes 1536008 | tf_op jit(solution)/shard_map/ppermute | solution.py:277
  148.0 5.8 %collective-permute-done.6.refs_6_ = bf16[1000,256]{1,0:T(8,128)(2,1)S(1)} collective-permute-done((bf16[1000,256]{1,0:T(8,128)(2,1)S(1)}, bf16[1000,256]{1,0:T(8,128)(2,1)S(1)}, u32[]{:S(2)}, u32[]{:S(2)}) %collective-permute-start.6) | collective-permute-done | bytes 512032 | tf_op jit(solution)/shard_map/ppermute | solution.py:275
  153.8 1.9 collective-permute-start.7
  155.7 0.0 collective-permute-done.14.refs_7_
  155.7 4.6 %collective-permute-start.15 = (bf16[1000,256]{1,0:T(8,128)(2,1)S(1)}, bf16[1000,256]{1,0:T(8,128)(2,1)S(1)}, u32[]{:S(2)}, u32[]{:S(2)}) collective-permute-start(bf16[1000,256]{1,0:T(8,128)(2,1)S(1)} %collective-permute-done.14.refs_7_), channel_id=1, source_target_pairs={{0,480},{32,0},{64,32},{96,64},{128,96},{160,128},{192,160},{224,1... | collective-permute-start | bytes 1536008 | tf_op jit(solution)/shard_map/ppermute | solution.py:277
  160.3 4.9 %collective-permute-done.7.refs_8_ = bf16[1000,256]{1,0:T(8,128)(2,1)S(1)} collective-permute-done((bf16[1000,256]{1,0:T(8,128)(2,1)S(1)}, bf16[1000,256]{1,0:T(8,128)(2,1)S(1)}, u32[]{:S(2)}, u32[]{:S(2)}) %collective-permute-start.7) | collective-permute-done | bytes 512032 | tf_op jit(solution)/shard_map/ppermute | solution.py:275
  165.3 1.9 collective-permute-start.8
  167.2 0.0 collective-permute-done.two_ref
  167.2 4.5 %norm.1 = (bf16[16,896,256]{2,1,0:T(8,128)(2,1)S(1)}, f32[2,16,16,128]{3,2,1,0:T(8,128)S(1)}) custom-call(bf16[16,912,128]{2,1,0:T(8,128)(2,1)S(1)} %all_to_all.16.one_ref, bf16[16,912,128]{2,1,0:T(8,128)(2,1)S(1)} %collective-permute-done.two_ref), custom_call_target="tpu_custom_call" | custom-call | flops 22413312 | bytes 14942208 | tf_op jit(solution)/shard_map/norm/pallas_call | solution.py:123
  171.6 2.9 %scores.2.refs_10_ = f32[1000,896]{1,0:T(8,128)S(1)} custom-call(bf16[16,896,256]{2,1,0:T(8,128)(2,1)S(1)} %get-tuple-element.8.n_ref, bf16[1000,256]{1,0:T(8,128)(2,1)S(1)} %bitcast.12, bf16[1000,256]{1,0:T(8,128)(2,1)S(1)} %collective-permute-done.1.refs_1_, bf16[1000,256]{1,0:T(8,128)(2,1)S(1)} %collective-permute-done.9.refs_2_, ...), custom_call_target="tpu_custom_call" | custom-call | flops 2293760000 | bytes 7168000 | tf_op jit(solution)/shard_map/scores/pallas_call | solution.py:169
  174.5 0.0 copy-start.1
  174.5 0.0 collective-permute-done.15.refs_9_
  174.5 5.5 %scores.3.acc_ref = f32[1000,896]{1,0:T(8,128)S(1)} custom-call(bf16[16,896,256]{2,1,0:T(8,128)(2,1)S(1)} %get-tuple-element.8.n_ref, bf16[1000,256]{1,0:T(8,128)(2,1)S(1)} %collective-permute-done.3.refs_0_, bf16[1000,256]{1,0:T(8,128)(2,1)S(1)} %collective-permute-done.11.refs_1_, ...), custom_call_target="tpu_custom_call", output_to_operand_aliasing={{}: (11, {})} | custom-call | flops 4587520000 | bytes 7168000 | tf_op jit(solution)/shard_map/scores/pallas_call | solution.py:169
  180.1 0.0 collective-permute-done.8.w_ref
  180.1 0.0 copy-done.1
  180.1 1.9 stats.1
  182.0 0.8 broadcast_in_dim.23
  182.9 9.3 %all-to-all-start.1 = ((f32[32,4,896]{2,1,0:T(4,128)}), f32[32,4,896]{2,1,0:T(4,128)S(1)}, u32[]{:S(2)}, u32[]{:S(2)}) async-start(f32[32,4,896]{2,1,0:T(4,128)} %broadcast_in_dim.23), calls=%async_computation.1 | async-start | bytes 917504 | tf_op jit(solution)/shard_map/all_to_all | solution.py:299
  192.2 0.1 convert_element_type.6.seq_ref
  192.4 0.1 squeeze.10.live_ref
  192.5 10.7 %all-to-all-done.1.x_ref = f32[32,4,896]{2,1,0:T(4,128)S(1)} async-done(((f32[32,4,896]{2,1,0:T(4,128)}), f32[32,4,896]{2,1,0:T(4,128)S(1)}, u32[]{:S(2)}, u32[]{:S(2)}) %all-to-all-start.1) | async-done | bytes 458784 | tf_op jit(solution)/shard_map/all_to_all | solution.py:299
  203.2 1.6 combine.1
  204.8 18.6 %all_to_all.17 = f32[16,1,128]{2,1,0:T(1,128)S(1)} all-to-all(f32[16,1,128]{2,1,0:T(1,128)S(1)} %broadcast_in_dim.24), channel_id=1, replica_groups=mesh['dp'=16,'tensor'=32] {'dp'}, dimensions={0} | all-to-all | bytes 16384 | tf_op jit(solution)/shard_map/all_to_all | solution.py:303
  223.4 0.6 maximum_divide_fusion
  (6 shorter events, 0.1 us)
Async XLA Ops:
  3.6 56.5 %copy-start = (bf16[256,1000]{0,1:T(8,128)(2,1)S(1)}, bf16[256,1000]{0,1:T(8,128)(2,1)}, u32[]{:S(2)}) copy-start(bf16[256,1000]{0,1:T(8,128)(2,1)} %param.8) | copy-start | bytes 1536004
  54.2 113.0 %collective-permute-start = (bf16[16,912,128]{2,1,0:T(8,128)(2,1)S(1)}, bf16[16,912,128]{2,1,0:T(8,128)(2,1)S(1)}, u32[]{:S(2)}, u32[]{:S(2)}) collective-permute-start(bf16[16,912,128]{2,1,0:T(8,128)(2,1)S(1)} %all_to_all.16.one_ref), channel_id=1, source_target_pairs={{0,1},{1,0},{2,3},{3,2},{4,5},{5,4},{6,7},{7,6},{8,9},{9,8},{10,11... | collective-permute-start | bytes 11206664 | tf_op jit(solution)/shard_map/ppermute | solution.py:286
  60.1 23.7 %collective-permute-start.1 = (bf16[1000,256]{1,0:T(8,128)(2,1)S(1)}, bf16[1000,256]{1,0:T(8,128)(2,1)S(1)}, u32[]{:S(2)}, u32[]{:S(2)}) collective-permute-start(bf16[1000,256]{1,0:T(8,128)(2,1)S(1)} %bitcast.10), channel_id=1, source_target_pairs={{0,32},{32,64},{64,96},{96,128},{128,160},{160,192},{192,224},{224... | collective-permute-start | bytes 1536008 | tf_op jit(solution)/shard_map/ppermute | solution.py:275
  64.2 21.5 %collective-permute-start.9 = (bf16[1000,256]{1,0:T(8,128)(2,1)S(1)}, bf16[1000,256]{1,0:T(8,128)(2,1)S(1)}, u32[]{:S(2)}, u32[]{:S(2)}) collective-permute-start(bf16[1000,256]{1,0:T(8,128)(2,1)S(1)} %bitcast.11), channel_id=1, source_target_pairs={{0,480},{32,0},{64,32},{96,64},{128,96},{160,128},{192,160},{224,1... | collective-permute-start | bytes 1536008 | tf_op jit(solution)/shard_map/ppermute | solution.py:277
  83.8 15.7 %collective-permute-start.2 = (bf16[1000,256]{1,0:T(8,128)(2,1)S(1)}, bf16[1000,256]{1,0:T(8,128)(2,1)S(1)}, u32[]{:S(2)}, u32[]{:S(2)}) collective-permute-start(bf16[1000,256]{1,0:T(8,128)(2,1)S(1)} %collective-permute-done.1.refs_1_), channel_id=1, source_target_pairs={{0,32},{32,64},{64,96},{96,128},{128,160},{160,192},{192,224},{224... | collective-permute-start | bytes 1536008 | tf_op jit(solution)/shard_map/ppermute | solution.py:275
  85.7 15.7 %collective-permute-start.10 = (bf16[1000,256]{1,0:T(8,128)(2,1)S(1)}, bf16[1000,256]{1,0:T(8,128)(2,1)S(1)}, u32[]{:S(2)}, u32[]{:S(2)}) collective-permute-start(bf16[1000,256]{1,0:T(8,128)(2,1)S(1)} %collective-permute-done.9.refs_2_), channel_id=1, source_target_pairs={{0,480},{32,0},{64,32},{96,64},{128,96},{160,128},{192,160},{224,1... | collective-permute-start | bytes 1536008 | tf_op jit(solution)/shard_map/ppermute | solution.py:277
  99.5 14.9 %collective-permute-start.3 = (bf16[1000,256]{1,0:T(8,128)(2,1)S(1)}, bf16[1000,256]{1,0:T(8,128)(2,1)S(1)}, u32[]{:S(2)}, u32[]{:S(2)}) collective-permute-start(bf16[1000,256]{1,0:T(8,128)(2,1)S(1)} %collective-permute-done.2.refs_3_), channel_id=1, source_target_pairs={{0,32},{32,64},{64,96},{96,128},{128,160},{160,192},{192,224},{224... | collective-permute-start | bytes 1536008 | tf_op jit(solution)/shard_map/ppermute | solution.py:275
  101.4 14.9 %collective-permute-start.11 = (bf16[1000,256]{1,0:T(8,128)(2,1)S(1)}, bf16[1000,256]{1,0:T(8,128)(2,1)S(1)}, u32[]{:S(2)}, u32[]{:S(2)}) collective-permute-start(bf16[1000,256]{1,0:T(8,128)(2,1)S(1)} %collective-permute-done.10.refs_4_), channel_id=1, source_target_pairs={{0,480},{32,0},{64,32},{96,64},{128,96},{160,128},{192,160},{224,1... | collective-permute-start | bytes 1536008 | tf_op jit(solution)/shard_map/ppermute | solution.py:277
  114.4 14.0 %collective-permute-start.4 = (bf16[1000,256]{1,0:T(8,128)(2,1)S(1)}, bf16[1000,256]{1,0:T(8,128)(2,1)S(1)}, u32[]{:S(2)}, u32[]{:S(2)}) collective-permute-start(bf16[1000,256]{1,0:T(8,128)(2,1)S(1)} %collective-permute-done.3.refs_0_), channel_id=1, source_target_pairs={{0,32},{32,64},{64,96},{96,128},{128,160},{160,192},{192,224},{224... | collective-permute-start | bytes 1536008 | tf_op jit(solution)/shard_map/ppermute | solution.py:275
  116.3 14.0 %collective-permute-start.12 = (bf16[1000,256]{1,0:T(8,128)(2,1)S(1)}, bf16[1000,256]{1,0:T(8,128)(2,1)S(1)}, u32[]{:S(2)}, u32[]{:S(2)}) collective-permute-start(bf16[1000,256]{1,0:T(8,128)(2,1)S(1)} %collective-permute-done.11.refs_1_), channel_id=1, source_target_pairs={{0,480},{32,0},{64,32},{96,64},{128,96},{160,128},{192,160},{224,1... | collective-permute-start | bytes 1536008 | tf_op jit(solution)/shard_map/ppermute | solution.py:277
  128.4 13.2 %collective-permute-start.5 = (bf16[1000,256]{1,0:T(8,128)(2,1)S(1)}, bf16[1000,256]{1,0:T(8,128)(2,1)S(1)}, u32[]{:S(2)}, u32[]{:S(2)}) collective-permute-start(bf16[1000,256]{1,0:T(8,128)(2,1)S(1)} %collective-permute-done.4.refs_2_), channel_id=1, source_target_pairs={{0,32},{32,64},{64,96},{96,128},{128,160},{160,192},{192,224},{224... | collective-permute-start | bytes 1536008 | tf_op jit(solution)/shard_map/ppermute | solution.py:275
  130.3 13.1 %collective-permute-start.13 = (bf16[1000,256]{1,0:T(8,128)(2,1)S(1)}, bf16[1000,256]{1,0:T(8,128)(2,1)S(1)}, u32[]{:S(2)}, u32[]{:S(2)}) collective-permute-start(bf16[1000,256]{1,0:T(8,128)(2,1)S(1)} %collective-permute-done.12.refs_3_), channel_id=1, source_target_pairs={{0,480},{32,0},{64,32},{96,64},{128,96},{160,128},{192,160},{224,1... | collective-permute-start | bytes 1536008 | tf_op jit(solution)/shard_map/ppermute | solution.py:277
  141.5 12.3 %collective-permute-start.6 = (bf16[1000,256]{1,0:T(8,128)(2,1)S(1)}, bf16[1000,256]{1,0:T(8,128)(2,1)S(1)}, u32[]{:S(2)}, u32[]{:S(2)}) collective-permute-start(bf16[1000,256]{1,0:T(8,128)(2,1)S(1)} %collective-permute-done.5.refs_4_), channel_id=1, source_target_pairs={{0,32},{32,64},{64,96},{96,128},{128,160},{160,192},{192,224},{224... | collective-permute-start | bytes 1536008 | tf_op jit(solution)/shard_map/ppermute | solution.py:275
  143.4 12.3 %collective-permute-start.14 = (bf16[1000,256]{1,0:T(8,128)(2,1)S(1)}, bf16[1000,256]{1,0:T(8,128)(2,1)S(1)}, u32[]{:S(2)}, u32[]{:S(2)}) collective-permute-start(bf16[1000,256]{1,0:T(8,128)(2,1)S(1)} %collective-permute-done.13.refs_5_), channel_id=1, source_target_pairs={{0,480},{32,0},{64,32},{96,64},{128,96},{160,128},{192,160},{224,1... | collective-permute-start | bytes 1536008 | tf_op jit(solution)/shard_map/ppermute | solution.py:277
  153.8 11.4 %collective-permute-start.7 = (bf16[1000,256]{1,0:T(8,128)(2,1)S(1)}, bf16[1000,256]{1,0:T(8,128)(2,1)S(1)}, u32[]{:S(2)}, u32[]{:S(2)}) collective-permute-start(bf16[1000,256]{1,0:T(8,128)(2,1)S(1)} %collective-permute-done.6.refs_6_), channel_id=1, source_target_pairs={{0,32},{32,64},{64,96},{96,128},{128,160},{160,192},{192,224},{224... | collective-permute-start | bytes 1536008 | tf_op jit(solution)/shard_map/ppermute | solution.py:275
  155.7 18.8 %collective-permute-start.15 = (bf16[1000,256]{1,0:T(8,128)(2,1)S(1)}, bf16[1000,256]{1,0:T(8,128)(2,1)S(1)}, u32[]{:S(2)}, u32[]{:S(2)}) collective-permute-start(bf16[1000,256]{1,0:T(8,128)(2,1)S(1)} %collective-permute-done.14.refs_7_), channel_id=1, source_target_pairs={{0,480},{32,0},{64,32},{96,64},{128,96},{160,128},{192,160},{224,1... | collective-permute-start | bytes 1536008 | tf_op jit(solution)/shard_map/ppermute | solution.py:277
  165.3 14.8 %collective-permute-start.8 = (bf16[1000,256]{1,0:T(8,128)(2,1)S(1)}, bf16[1000,256]{1,0:T(8,128)(2,1)S(1)}, u32[]{:S(2)}, u32[]{:S(2)}) collective-permute-start(bf16[1000,256]{1,0:T(8,128)(2,1)S(1)} %collective-permute-done.7.refs_8_), channel_id=1, source_target_pairs={{0,32},{32,64},{64,96},{96,128},{128,160},{160,192},{192,224},{224... | collective-permute-start | bytes 1536008 | tf_op jit(solution)/shard_map/ppermute | solution.py:275
  174.5 5.6 %copy-start.1 = (s32[896]{0:T(1024)S(1)}, s32[896]{0:T(1024)}, u32[]{:S(2)}) copy-start(s32[896]{0:T(1024)} %ids_ref.1) | copy-start | bytes 10756
  182.9 20.3 %all-to-all-start.1 = ((f32[32,4,896]{2,1,0:T(4,128)}), f32[32,4,896]{2,1,0:T(4,128)S(1)}, u32[]{:S(2)}, u32[]{:S(2)}) async-start(f32[32,4,896]{2,1,0:T(4,128)} %broadcast_in_dim.23), calls=%async_computation.1 | async-start | bytes 917504 | tf_op jit(solution)/shard_map/all_to_all | solution.py:299

commit v5 on v4

--- a/solution.py
+++ b/solution.py
@@ -178,7 +178,7 @@
     )(normed, *ws, *([] if acc is None else [acc]))
 
 
-def stats_kernel(ahead, n_ref, w_ref, acc_ref, ids_ref, out_ref, s_ref):
+def stats_kernel(ahead, n_ref, w_ref, acc_ref, ids_ref, copies_ref, s_ref, out_ref, sems):
     vocab, tokens = acc_ref.shape
     at = row_block(ahead)
     first = lax.axis_index("tensor") * vocab
@@ -198,20 +198,40 @@
         out_ref[1:2, at] = total
         out_ref[2:3, at] = spread
         out_ref[3:4, at] = picked
-
-
-def statistics(ahead, normed, w, acc, ids):
+    moves = [
+        pltpu.make_async_copy(out_ref, copies_ref.at[i], sems.at[i])
+        for i in range(copies_ref.shape[0])
+    ]
+    for move in moves:
+        move.start()
+    for move in moves:
+        move.wait()
+
+
+def statistics(ahead, normed, w, acc, ids, copies):
     vocab, tokens = acc.shape
     return pl.pallas_call(
         functools.partial(stats_kernel, ahead),
-        out_shape=jax.ShapeDtypeStruct((4, tokens), jnp.float32),
+        out_shape=pltpu.HBM((copies, 4, tokens), jnp.float32),
         in_specs=[VM] * 4,
-        out_specs=VM,
-        scratch_shapes=[pltpu.VMEM((vocab, tokens), jnp.float32)],
+        out_specs=pl.BlockSpec(memory_space=pltpu.HBM),
+        scratch_shapes=[
+            pltpu.VMEM((vocab, tokens), jnp.float32),
+            pltpu.VMEM((4, tokens), jnp.float32),
+            pltpu.SemaphoreType.DMA((copies,)),
+        ],
         compiler_params=room(12),
         cost_estimate=cost(2 * vocab * w.shape[1] * tokens, 8 * vocab * tokens),
         name="stats",
     )(normed, w, acc, ids)
+
+
+exact = functools.partial(
+    lax.dot_general,
+    dimension_numbers=NT,
+    precision=lax.Precision.HIGHEST,
+    preferred_element_type=jnp.float32,
+)
 
 
 def combine_kernel(x_ref, seq_ref, live_ref, logprob_ref, entropy_ref, sums_ref):
@@ -226,30 +246,19 @@
     live = live_ref[...]
     log_total = jnp.log(g_total)
     logprob = (g_target - best - log_total) * live
-    entropy = (log_total - g_spread / g_total) * live
+    logprob_ref[...] = logprob
+    entropy_ref[...] = (log_total - g_spread / g_total) * live
     tokens = top.shape[1]
-    share = logprob_ref.shape[1]
     row = lax.broadcasted_iota(jnp.int32, (8, tokens), 0)
-    rows = jnp.where(row == 0, logprob, jnp.where(row == 1, live, jnp.where(row == 2, entropy, 0.0)))
+    rows = jnp.where(row == 0, logprob, jnp.where(row == 1, live, 0.0))
     seat = lax.broadcasted_iota(jnp.int32, (2 * SEQS, tokens), 0)
-    member = (seat % SEQS == seq_ref[...]).astype(jnp.float32)
-    token = lax.broadcasted_iota(jnp.int32, (2 * SEQS, tokens), 1)
-    mine = (token == seat + lax.axis_index("tensor") * share).astype(jnp.float32)
-    exact = functools.partial(
-        lax.dot_general,
-        dimension_numbers=NT,
-        precision=lax.Precision.HIGHEST,
-        preferred_element_type=jnp.float32,
-    )
-    sums, own = exact(rows, member), exact(rows, mine)
+    sums = exact(rows, (seat % SEQS == seq_ref[...]).astype(jnp.float32))
     lane = lax.broadcasted_iota(jnp.int32, (1, 2 * SEQS), 1)
     sums_ref[...] = jnp.where(lane < SEQS, sums[0:1, :], sums[1:2, :])
-    logprob_ref[...] = own[0:1, 0:share]
-    entropy_ref[...] = own[2:3, 0:share]
 
 
 def combine(x, seq, live):
-    row = jax.ShapeDtypeStruct((1, x.shape[2] // x.shape[0]), jnp.float32)
+    row = jax.ShapeDtypeStruct((1, x.shape[2]), jnp.float32)
     return pl.pallas_call(
         combine_kernel,
         out_shape=(row, row, jax.ShapeDtypeStruct((1, 2 * SEQS), jnp.float32)),
@@ -258,6 +267,29 @@
         compiler_params=room(8),
         name="combine",
     )(x, seq, live)
+
+
+def pick_kernel(logprob_ref, entropy_ref, own_logprob_ref, own_entropy_ref):
+    tokens, share = logprob_ref.shape[1], own_logprob_ref.shape[1]
+    row = lax.broadcasted_iota(jnp.int32, (8, tokens), 0)
+    rows = jnp.where(row == 0, logprob_ref[...], jnp.where(row == 1, entropy_ref[...], 0.0))
+    seat = lax.broadcasted_iota(jnp.int32, (128, tokens), 0)
+    token = lax.broadcasted_iota(jnp.int32, (128, tokens), 1)
+    own = exact(rows, (token == seat + lax.axis_index("tensor") * share).astype(jnp.float32))
+    own_logprob_ref[...] = own[0:1, 0:share]
+    own_entropy_ref[...] = own[1:2, 0:share]
+
+
+def pick(logprob, entropy, share):
+    own = jax.ShapeDtypeStruct((1, share), jnp.float32)
+    return pl.pallas_call(
+        pick_kernel,
+        out_shape=(own, own),
+        in_specs=[VM] * 2,
+        out_specs=(VM, VM),
+        compiler_params=room(8),
+        name="pick",
+    )(logprob, entropy)
 
 
 def body(hidden, gain, head_weight, targets, seq_ids, live):
@@ -294,16 +326,15 @@
     acc = accumulate(aheads[5:15], normed, chunks[5:15], acc)
     flags = extra[:, :, 1:3, :share].transpose(2, 1, 0, 3).reshape(2, 1, tokens)
     seq, alive = flags[0].astype(jnp.int32), flags[1]
-    stats = statistics(ring // 2, normed, last, acc, targets)
-
-    everyone = lax.all_to_all(
-        jnp.broadcast_to(stats[None], (shards, *stats.shape)), "tensor", 0, 0
-    )
+    stats = statistics(ring // 2, normed, last, acc, targets, shards)
+
+    everyone = lax.all_to_all(stats, "tensor", 0, 0)
     logprob, entropy, sums = combine(everyone, seq, alive)
     planes = lax.all_to_all(jnp.broadcast_to(sums, (ring, 2 * SEQS)), "dp", 0, 0)
     whole = jnp.sum(planes, axis=0)
     seq_mean = whole[:SEQS] / jnp.maximum(whole[SEQS:], 1.0)
-    return logprob[0], entropy[0], seq_mean
+    own_logprob, own_entropy = pick(logprob, entropy, share)
+    return own_logprob[0], own_entropy[0], seq_mean
 
 
 def solution(mesh):

time: 225 us -> 225 us (level)
  blocking collectives: 69.1 us -> 50.6 us
  waiting for transfers between devices: 63.3 us -> 73.5 us
  starting transfers between devices: 69.6 us -> 77 us
    all_to_all x1 -> x0, blocking collectives: 18.6 us -> none  [body(): lax.all_to_all(jnp.broadcast_to(sums, (ring, 2 * SEQS)), 'dp', 0, 0)]
    all_to_all x1 -> x2, waiting for transfers between devices: 10.7 us -> 20.9 us  [the longest x1 10.7 us: body(): everyone = lax.all_to_all(stats, 'tensor', 0, 0)]
    all_to_all x1 -> x2, starting transfers between devices: 9.28 us -> 16.7 us  [the longest x1 9.28 us: body(): everyone = lax.all_to_all(stats, 'tensor', 0, 0)]
  transfers between devices with their start and end apart: 17 -> 18, of which waited for: 8 -> 9; matrix products, arithmetic and copies ran while one was open for 0% -> 0% of each run, Pallas kernels for 6% -> 6%
where the time goes in v5:
time: 225 us; the launch traced here: 224 us
  starting transfers between devices  77 us (34%)
  waiting for transfers between devices  73.5 us (33%)
  blocking collectives  50.6 us (22%)
  Pallas kernels  20.4 us (9%)
    ppermute x8, waiting for transfers between devices, turn(): a = lax.ppermute(a, 'dp', forth)  52.5 us
    all_to_all x1, blocking collectives, body(): one = lax.all_to_all(sent, 'tensor', 0, 0, axis_index_groups=teams)  50.6 us
    ppermute x7, starting transfers between devices, turn(): b = lax.ppermute(b, 'dp', back)  36.9 us
    ppermute x8, starting transfers between devices, turn(): a = lax.ppermute(a, 'dp', forth)  17.4 us
    all_to_all x1, waiting for transfers between devices, body(): everyone = lax.all_to_all(stats, 'tensor', 0, 0)  10.7 us
    all_to_all x1, waiting for transfers between devices, body(): lax.all_to_all(jnp.broadcast_to(sums, (ring, 2 * SEQS)), 'dp', 0, 0)  10.2 us
    all_to_all x1, starting transfers between devices, body(): everyone = lax.all_to_all(stats, 'tensor', 0, 0)  9.28 us
    pallas_call x2, Pallas kernels, accumulate(): pl.pallas_call(functools.partial(mm_kernel, tuple(aheads)), out_shape=jax...  8.42 us
  transfers between devices with their start and end apart: 18, of which 9 were waited for; matrix products, arithmetic and copies ran while one was open for 0% of the time, Pallas kernels for 6%

profile of v5, /device:TPU:1, one launch (start us, length us, event | category | flops | bytes accessed | tf_op | source)
XLA Modules:
  0.0 224.0 jit_solution(286636790906645367)
XLA Ops:
  0.6 2.9 %fan.1 = bf16[16,912,128]{2,1,0:T(8,128)(2,1)} custom-call(bf16[896,128]{1,0:T(8,128)(2,1)} %hid_ref.1, bf16[1,128]{1,0:T(2,128)(2,1)} %bitcast.15, s32[1,28]{1,0:T(1,128)} %bitcast.16, s32[1,28]{1,0:T(1,128)} %bitcast.17), custom_call_target="tpu_custom_call" | custom-call | tf_op jit(solution)/shard_map/fan/pallas_call | solution.py:53
  3.6 0.0 copy-start
  3.6 50.6 %all_to_all.16.one_ref = bf16[16,912,128]{2,1,0:T(8,128)(2,1)S(1)} all-to-all(bf16[16,912,128]{2,1,0:T(8,128)(2,1)} %fan.1), channel_id=1, replica_groups={{0,2,4,6,8,10,12,14,16,18,20,22,24,26,28,30},{1,3,5,7,9,11,13,15,17,19,..., dimensions={0} | all-to-all | bytes 7471104 | tf_op jit(solution)/shard_map/all_to_all | solution.py:317
  54.2 5.9 %collective-permute-start = (bf16[16,912,128]{2,1,0:T(8,128)(2,1)S(1)}, bf16[16,912,128]{2,1,0:T(8,128)(2,1)S(1)}, u32[]{:S(2)}, u32[]{:S(2)}) collective-permute-start(bf16[16,912,128]{2,1,0:T(8,128)(2,1)S(1)} %all_to_all.16.one_ref), channel_id=1, source_target_pairs={{0,1},{1,0},{2,3},{3,2},{4,5},{5,4},{6,7},{7,6},{8,9},{9,8},{10,11... | collective-permute-start | bytes 11206664 | tf_op jit(solution)/shard_map/ppermute | solution.py:318
  60.1 0.0 copy-done
  60.1 4.1 %collective-permute-start.1 = (bf16[1000,256]{1,0:T(8,128)(2,1)S(1)}, bf16[1000,256]{1,0:T(8,128)(2,1)S(1)}, u32[]{:S(2)}, u32[]{:S(2)}) collective-permute-start(bf16[1000,256]{1,0:T(8,128)(2,1)S(1)} %bitcast.10), channel_id=1, source_target_pairs={{0,32},{32,64},{64,96},{96,128},{128,160},{160,192},{192,224},{224... | collective-permute-start | bytes 1536008 | tf_op jit(solution)/shard_map/ppermute | solution.py:307
  64.2 9.5 %collective-permute-start.9 = (bf16[1000,256]{1,0:T(8,128)(2,1)S(1)}, bf16[1000,256]{1,0:T(8,128)(2,1)S(1)}, u32[]{:S(2)}, u32[]{:S(2)}) collective-permute-start(bf16[1000,256]{1,0:T(8,128)(2,1)S(1)} %bitcast.11), channel_id=1, source_target_pairs={{0,480},{32,0},{64,32},{96,64},{128,96},{160,128},{192,160},{224,1... | collective-permute-start | bytes 1536008 | tf_op jit(solution)/shard_map/ppermute | solution.py:309
  73.7 10.1 %collective-permute-done.1.refs_1_ = bf16[1000,256]{1,0:T(8,128)(2,1)S(1)} collective-permute-done((bf16[1000,256]{1,0:T(8,128)(2,1)S(1)}, bf16[1000,256]{1,0:T(8,128)(2,1)S(1)}, u32[]{:S(2)}, u32[]{:S(2)}) %collective-permute-start.1) | collective-permute-done | bytes 512032 | tf_op jit(solution)/shard_map/ppermute | solution.py:307
  83.8 1.9 collective-permute-start.2
  85.7 0.0 collective-permute-done.9.refs_2_
  85.7 4.6 %collective-permute-start.10 = (bf16[1000,256]{1,0:T(8,128)(2,1)S(1)}, bf16[1000,256]{1,0:T(8,128)(2,1)S(1)}, u32[]{:S(2)}, u32[]{:S(2)}) collective-permute-start(bf16[1000,256]{1,0:T(8,128)(2,1)S(1)} %collective-permute-done.9.refs_2_), channel_id=1, source_target_pairs={{0,480},{32,0},{64,32},{96,64},{128,96},{160,128},{192,160},{224,1... | collective-permute-start | bytes 1536008 | tf_op jit(solution)/shard_map/ppermute | solution.py:309
  90.3 9.2 %collective-permute-done.2.refs_3_ = bf16[1000,256]{1,0:T(8,128)(2,1)S(1)} collective-permute-done((bf16[1000,256]{1,0:T(8,128)(2,1)S(1)}, bf16[1000,256]{1,0:T(8,128)(2,1)S(1)}, u32[]{:S(2)}, u32[]{:S(2)}) %collective-permute-start.2) | collective-permute-done | bytes 512032 | tf_op jit(solution)/shard_map/ppermute | solution.py:307
  99.5 1.9 collective-permute-start.3
  101.4 0.0 collective-permute-done.10.refs_4_
  101.4 4.6 %collective-permute-start.11 = (bf16[1000,256]{1,0:T(8,128)(2,1)S(1)}, bf16[1000,256]{1,0:T(8,128)(2,1)S(1)}, u32[]{:S(2)}, u32[]{:S(2)}) collective-permute-start(bf16[1000,256]{1,0:T(8,128)(2,1)S(1)} %collective-permute-done.10.refs_4_), channel_id=1, source_target_pairs={{0,480},{32,0},{64,32},{96,64},{128,96},{160,128},{192,160},{224,1... | collective-permute-start | bytes 1536008 | tf_op jit(solution)/shard_map/ppermute | solution.py:309
  106.0 8.4 %collective-permute-done.3.refs_0_ = bf16[1000,256]{1,0:T(8,128)(2,1)S(1)} collective-permute-done((bf16[1000,256]{1,0:T(8,128)(2,1)S(1)}, bf16[1000,256]{1,0:T(8,128)(2,1)S(1)}, u32[]{:S(2)}, u32[]{:S(2)}) %collective-permute-start.3) | collective-permute-done | bytes 512032 | tf_op jit(solution)/shard_map/ppermute | solution.py:307
  114.4 1.9 collective-permute-start.4
  116.3 0.0 collective-permute-done.11.refs_1_
  116.3 4.6 %collective-permute-start.12 = (bf16[1000,256]{1,0:T(8,128)(2,1)S(1)}, bf16[1000,256]{1,0:T(8,128)(2,1)S(1)}, u32[]{:S(2)}, u32[]{:S(2)}) collective-permute-start(bf16[1000,256]{1,0:T(8,128)(2,1)S(1)} %collective-permute-done.11.refs_1_), channel_id=1, source_target_pairs={{0,480},{32,0},{64,32},{96,64},{128,96},{160,128},{192,160},{224,1... | collective-permute-start | bytes 1536008 | tf_op jit(solution)/shard_map/ppermute | solution.py:309
  120.9 7.5 %collective-permute-done.4.refs_2_ = bf16[1000,256]{1,0:T(8,128)(2,1)S(1)} collective-permute-done((bf16[1000,256]{1,0:T(8,128)(2,1)S(1)}, bf16[1000,256]{1,0:T(8,128)(2,1)S(1)}, u32[]{:S(2)}, u32[]{:S(2)}) %collective-permute-start.4) | collective-permute-done | bytes 512032 | tf_op jit(solution)/shard_map/ppermute | solution.py:307
  128.4 1.9 collective-permute-start.5
  130.3 0.0 collective-permute-done.12.refs_3_
  130.3 4.6 %collective-permute-start.13 = (bf16[1000,256]{1,0:T(8,128)(2,1)S(1)}, bf16[1000,256]{1,0:T(8,128)(2,1)S(1)}, u32[]{:S(2)}, u32[]{:S(2)}) collective-permute-start(bf16[1000,256]{1,0:T(8,128)(2,1)S(1)} %collective-permute-done.12.refs_3_), channel_id=1, source_target_pairs={{0,480},{32,0},{64,32},{96,64},{128,96},{160,128},{192,160},{224,1... | collective-permute-start | bytes 1536008 | tf_op jit(solution)/shard_map/ppermute | solution.py:309
  134.9 6.6 %collective-permute-done.5.refs_4_ = bf16[1000,256]{1,0:T(8,128)(2,1)S(1)} collective-permute-done((bf16[1000,256]{1,0:T(8,128)(2,1)S(1)}, bf16[1000,256]{1,0:T(8,128)(2,1)S(1)}, u32[]{:S(2)}, u32[]{:S(2)}) %collective-permute-start.5) | collective-permute-done | bytes 512032 | tf_op jit(solution)/shard_map/ppermute | solution.py:307
  141.5 1.9 collective-permute-start.6
  143.4 0.0 collective-permute-done.13.refs_5_
  143.4 4.6 %collective-permute-start.14 = (bf16[1000,256]{1,0:T(8,128)(2,1)S(1)}, bf16[1000,256]{1,0:T(8,128)(2,1)S(1)}, u32[]{:S(2)}, u32[]{:S(2)}) collective-permute-start(bf16[1000,256]{1,0:T(8,128)(2,1)S(1)} %collective-permute-done.13.refs_5_), channel_id=1, source_target_pairs={{0,480},{32,0},{64,32},{96,64},{128,96},{160,128},{192,160},{224,1... | collective-permute-start | bytes 1536008 | tf_op jit(solution)/shard_map/ppermute | solution.py:309
  148.0 5.8 %collective-permute-done.6.refs_6_ = bf16[1000,256]{1,0:T(8,128)(2,1)S(1)} collective-permute-done((bf16[1000,256]{1,0:T(8,128)(2,1)S(1)}, bf16[1000,256]{1,0:T(8,128)(2,1)S(1)}, u32[]{:S(2)}, u32[]{:S(2)}) %collective-permute-start.6) | collective-permute-done | bytes 512032 | tf_op jit(solution)/shard_map/ppermute | solution.py:307
  153.8 1.9 collective-permute-start.7
  155.7 0.0 collective-permute-done.14.refs_7_
  155.7 4.6 %collective-permute-start.15 = (bf16[1000,256]{1,0:T(8,128)(2,1)S(1)}, bf16[1000,256]{1,0:T(8,128)(2,1)S(1)}, u32[]{:S(2)}, u32[]{:S(2)}) collective-permute-start(bf16[1000,256]{1,0:T(8,128)(2,1)S(1)} %collective-permute-done.14.refs_7_), channel_id=1, source_target_pairs={{0,480},{32,0},{64,32},{96,64},{128,96},{160,128},{192,160},{224,1... | collective-permute-start | bytes 1536008 | tf_op jit(solution)/shard_map/ppermute | solution.py:309
  160.3 4.9 %collective-permute-done.7.refs_8_ = bf16[1000,256]{1,0:T(8,128)(2,1)S(1)} collective-permute-done((bf16[1000,256]{1,0:T(8,128)(2,1)S(1)}, bf16[1000,256]{1,0:T(8,128)(2,1)S(1)}, u32[]{:S(2)}, u32[]{:S(2)}) %collective-permute-start.7) | collective-permute-done | bytes 512032 | tf_op jit(solution)/shard_map/ppermute | solution.py:307
  165.3 1.9 collective-permute-start.8
  167.2 0.0 collective-permute-done.two_ref
  167.2 4.3 %norm.1 = (bf16[16,896,256]{2,1,0:T(8,128)(2,1)S(1)}, f32[2,16,16,128]{3,2,1,0:T(8,128)S(1)}) custom-call(bf16[16,912,128]{2,1,0:T(8,128)(2,1)S(1)} %all_to_all.16.one_ref, bf16[16,912,128]{2,1,0:T(8,128)(2,1)S(1)} %collective-permute-done.two_ref), custom_call_target="tpu_custom_call" | custom-call | flops 22413312 | bytes 14942208 | tf_op jit(solution)/shard_map/norm/pallas_call | solution.py:123
  171.5 2.9 %scores.2.refs_10_ = f32[1000,896]{1,0:T(8,128)S(1)} custom-call(bf16[16,896,256]{2,1,0:T(8,128)(2,1)S(1)} %get-tuple-element.10.n_ref, bf16[1000,256]{1,0:T(8,128)(2,1)S(1)} %bitcast.12, bf16[1000,256]{1,0:T(8,128)(2,1)S(1)} %collective-permute-done.1.refs_1_, bf16[1000,256]{1,0:T(8,128)(2,1)S(1)} %collective-permute-done.9.refs_2_, ...), custom_call_target="tpu_custom_call" | custom-call | flops 2293760000 | bytes 7168000 | tf_op jit(solution)/shard_map/scores/pallas_call | solution.py:169
  174.4 0.0 copy-start.1
  174.4 0.0 collective-permute-done.15.refs_9_
  174.4 5.5 %scores.3.acc_ref = f32[1000,896]{1,0:T(8,128)S(1)} custom-call(bf16[16,896,256]{2,1,0:T(8,128)(2,1)S(1)} %get-tuple-element.10.n_ref, bf16[1000,256]{1,0:T(8,128)(2,1)S(1)} %collective-permute-done.3.refs_0_, bf16[1000,256]{1,0:T(8,128)(2,1)S(1)} %collective-permute-done.11.refs_1_, ...), custom_call_target="tpu_custom_call", output_to_operand_aliasing={{}: (11, {})} | custom-call | flops 4587520000 | bytes 7168000 | tf_op jit(solution)/shard_map/scores/pallas_call | solution.py:169
  180.0 0.0 collective-permute-done.8.w_ref
  180.0 0.0 copy-done.1
  180.0 3.0 %stats.1 = f32[32,4,896]{2,1,0:T(4,128)} custom-call(bf16[16,896,256]{2,1,0:T(8,128)(2,1)S(1)} %get-tuple-element.10.n_ref, bf16[1000,256]{1,0:T(8,128)(2,1)S(1)} %collective-permute-done.8.w_ref, f32[1000,896]{1,0:T(8,128)S(1)} %scores.3.acc_ref, s32[896]{0:T(1024)S(1)} %copy-done.1), custom_call_target="tpu_custom_call" | custom-call | flops 458752000 | bytes 7168000 | tf_op jit(solution)/shard_map/stats/pallas_call | solution.py:213
  183.0 9.3 %all-to-all-start.1 = ((f32[32,4,896]{2,1,0:T(4,128)}), f32[32,4,896]{2,1,0:T(4,128)S(1)}, u32[]{:S(2)}, u32[]{:S(2)}) async-start(f32[32,4,896]{2,1,0:T(4,128)} %stats.1), calls=%async_computation.1 | async-start | bytes 917504 | tf_op jit(solution)/shard_map/all_to_all | solution.py:331
  192.3 0.1 convert_element_type.6.seq_ref
  192.5 0.1 squeeze.10.live_ref
  192.6 10.7 %all-to-all-done.1.x_ref = f32[32,4,896]{2,1,0:T(4,128)S(1)} async-done(((f32[32,4,896]{2,1,0:T(4,128)}), f32[32,4,896]{2,1,0:T(4,128)S(1)}, u32[]{:S(2)}, u32[]{:S(2)}) %all-to-all-start.1) | async-done | bytes 458784 | tf_op jit(solution)/shard_map/all_to_all | solution.py:331
  203.3 0.7 combine.1
  204.0 0.6 broadcast_in_dim.17
  204.6 7.5 %all-to-all-start.2 = ((f32[16,1,128]{2,1,0:T(1,128)}), f32[16,1,128]{2,1,0:T(1,128)S(1)}, u32[]{:S(2)}, u32[]{:S(2)}) async-start(f32[16,1,128]{2,1,0:T(1,128)} %broadcast_in_dim.17), calls=%async_computation.2 | async-start | bytes 16384 | tf_op jit(solution)/shard_map/all_to_all | solution.py:333
  212.1 1.1 pick.1
  213.1 10.2 %all-to-all-done.2 = f32[16,1,128]{2,1,0:T(1,128)S(1)} async-done(((f32[16,1,128]{2,1,0:T(1,128)}), f32[16,1,128]{2,1,0:T(1,128)S(1)}, u32[]{:S(2)}, u32[]{:S(2)}) %all-to-all-start.2) | async-done | bytes 8224 | tf_op jit(solution)/shard_map/all_to_all | solution.py:333
  223.4 0.6 maximum_divide_fusion
  (5 shorter events, 0.1 us)
Async XLA Ops:
  3.6 56.5 %copy-start = (bf16[256,1000]{0,1:T(8,128)(2,1)S(1)}, bf16[256,1000]{0,1:T(8,128)(2,1)}, u32[]{:S(2)}) copy-start(bf16[256,1000]{0,1:T(8,128)(2,1)} %param.8) | copy-start | bytes 1536004
  54.2 113.0 %collective-permute-start = (bf16[16,912,128]{2,1,0:T(8,128)(2,1)S(1)}, bf16[16,912,128]{2,1,0:T(8,128)(2,1)S(1)}, u32[]{:S(2)}, u32[]{:S(2)}) collective-permute-start(bf16[16,912,128]{2,1,0:T(8,128)(2,1)S(1)} %all_to_all.16.one_ref), channel_id=1, source_target_pairs={{0,1},{1,0},{2,3},{3,2},{4,5},{5,4},{6,7},{7,6},{8,9},{9,8},{10,11... | collective-permute-start | bytes 11206664 | tf_op jit(solution)/shard_map/ppermute | solution.py:318
  60.1 23.7 %collective-permute-start.1 = (bf16[1000,256]{1,0:T(8,128)(2,1)S(1)}, bf16[1000,256]{1,0:T(8,128)(2,1)S(1)}, u32[]{:S(2)}, u32[]{:S(2)}) collective-permute-start(bf16[1000,256]{1,0:T(8,128)(2,1)S(1)} %bitcast.10), channel_id=1, source_target_pairs={{0,32},{32,64},{64,96},{96,128},{128,160},{160,192},{192,224},{224... | collective-permute-start | bytes 1536008 | tf_op jit(solution)/shard_map/ppermute | solution.py:307
  64.2 21.5 %collective-permute-start.9 = (bf16[1000,256]{1,0:T(8,128)(2,1)S(1)}, bf16[1000,256]{1,0:T(8,128)(2,1)S(1)}, u32[]{:S(2)}, u32[]{:S(2)}) collective-permute-start(bf16[1000,256]{1,0:T(8,128)(2,1)S(1)} %bitcast.11), channel_id=1, source_target_pairs={{0,480},{32,0},{64,32},{96,64},{128,96},{160,128},{192,160},{224,1... | collective-permute-start | bytes 1536008 | tf_op jit(solution)/shard_map/ppermute | solution.py:309
  83.8 15.7 %collective-permute-start.2 = (bf16[1000,256]{1,0:T(8,128)(2,1)S(1)}, bf16[1000,256]{1,0:T(8,128)(2,1)S(1)}, u32[]{:S(2)}, u32[]{:S(2)}) collective-permute-start(bf16[1000,256]{1,0:T(8,128)(2,1)S(1)} %collective-permute-done.1.refs_1_), channel_id=1, source_target_pairs={{0,32},{32,64},{64,96},{96,128},{128,160},{160,192},{192,224},{224... | collective-permute-start | bytes 1536008 | tf_op jit(solution)/shard_map/ppermute | solution.py:307
  85.7 15.7 %collective-permute-start.10 = (bf16[1000,256]{1,0:T(8,128)(2,1)S(1)}, bf16[1000,256]{1,0:T(8,128)(2,1)S(1)}, u32[]{:S(2)}, u32[]{:S(2)}) collective-permute-start(bf16[1000,256]{1,0:T(8,128)(2,1)S(1)} %collective-permute-done.9.refs_2_), channel_id=1, source_target_pairs={{0,480},{32,0},{64,32},{96,64},{128,96},{160,128},{192,160},{224,1... | collective-permute-start | bytes 1536008 | tf_op jit(solution)/shard_map/ppermute | solution.py:309
  99.5 14.9 %collective-permute-start.3 = (bf16[1000,256]{1,0:T(8,128)(2,1)S(1)}, bf16[1000,256]{1,0:T(8,128)(2,1)S(1)}, u32[]{:S(2)}, u32[]{:S(2)}) collective-permute-start(bf16[1000,256]{1,0:T(8,128)(2,1)S(1)} %collective-permute-done.2.refs_3_), channel_id=1, source_target_pairs={{0,32},{32,64},{64,96},{96,128},{128,160},{160,192},{192,224},{224... | collective-permute-start | bytes 1536008 | tf_op jit(solution)/shard_map/ppermute | solution.py:307
  101.4 14.9 %collective-permute-start.11 = (bf16[1000,256]{1,0:T(8,128)(2,1)S(1)}, bf16[1000,256]{1,0:T(8,128)(2,1)S(1)}, u32[]{:S(2)}, u32[]{:S(2)}) collective-permute-start(bf16[1000,256]{1,0:T(8,128)(2,1)S(1)} %collective-permute-done.10.refs_4_), channel_id=1, source_target_pairs={{0,480},{32,0},{64,32},{96,64},{128,96},{160,128},{192,160},{224,1... | collective-permute-start | bytes 1536008 | tf_op jit(solution)/shard_map/ppermute | solution.py:309
  114.4 14.0 %collective-permute-start.4 = (bf16[1000,256]{1,0:T(8,128)(2,1)S(1)}, bf16[1000,256]{1,0:T(8,128)(2,1)S(1)}, u32[]{:S(2)}, u32[]{:S(2)}) collective-permute-start(bf16[1000,256]{1,0:T(8,128)(2,1)S(1)} %collective-permute-done.3.refs_0_), channel_id=1, source_target_pairs={{0,32},{32,64},{64,96},{96,128},{128,160},{160,192},{192,224},{224... | collective-permute-start | bytes 1536008 | tf_op jit(solution)/shard_map/ppermute | solution.py:307
  116.3 14.0 %collective-permute-start.12 = (bf16[1000,256]{1,0:T(8,128)(2,1)S(1)}, bf16[1000,256]{1,0:T(8,128)(2,1)S(1)}, u32[]{:S(2)}, u32[]{:S(2)}) collective-permute-start(bf16[1000,256]{1,0:T(8,128)(2,1)S(1)} %collective-permute-done.11.refs_1_), channel_id=1, source_target_pairs={{0,480},{32,0},{64,32},{96,64},{128,96},{160,128},{192,160},{224,1... | collective-permute-start | bytes 1536008 | tf_op jit(solution)/shard_map/ppermute | solution.py:309
  128.4 13.2 %collective-permute-start.5 = (bf16[1000,256]{1,0:T(8,128)(2,1)S(1)}, bf16[1000,256]{1,0:T(8,128)(2,1)S(1)}, u32[]{:S(2)}, u32[]{:S(2)}) collective-permute-start(bf16[1000,256]{1,0:T(8,128)(2,1)S(1)} %collective-permute-done.4.refs_2_), channel_id=1, source_target_pairs={{0,32},{32,64},{64,96},{96,128},{128,160},{160,192},{192,224},{224... | collective-permute-start | bytes 1536008 | tf_op jit(solution)/shard_map/ppermute | solution.py:307
  130.3 13.1 %collective-permute-start.13 = (bf16[1000,256]{1,0:T(8,128)(2,1)S(1)}, bf16[1000,256]{1,0:T(8,128)(2,1)S(1)}, u32[]{:S(2)}, u32[]{:S(2)}) collective-permute-start(bf16[1000,256]{1,0:T(8,128)(2,1)S(1)} %collective-permute-done.12.refs_3_), channel_id=1, source_target_pairs={{0,480},{32,0},{64,32},{96,64},{128,96},{160,128},{192,160},{224,1... | collective-permute-start | bytes 1536008 | tf_op jit(solution)/shard_map/ppermute | solution.py:309
  141.5 12.3 %collective-permute-start.6 = (bf16[1000,256]{1,0:T(8,128)(2,1)S(1)}, bf16[1000,256]{1,0:T(8,128)(2,1)S(1)}, u32[]{:S(2)}, u32[]{:S(2)}) collective-permute-start(bf16[1000,256]{1,0:T(8,128)(2,1)S(1)} %collective-permute-done.5.refs_4_), channel_id=1, source_target_pairs={{0,32},{32,64},{64,96},{96,128},{128,160},{160,192},{192,224},{224... | collective-permute-start | bytes 1536008 | tf_op jit(solution)/shard_map/ppermute | solution.py:307
  143.4 12.3 %collective-permute-start.14 = (bf16[1000,256]{1,0:T(8,128)(2,1)S(1)}, bf16[1000,256]{1,0:T(8,128)(2,1)S(1)}, u32[]{:S(2)}, u32[]{:S(2)}) collective-permute-start(bf16[1000,256]{1,0:T(8,128)(2,1)S(1)} %collective-permute-done.13.refs_5_), channel_id=1, source_target_pairs={{0,480},{32,0},{64,32},{96,64},{128,96},{160,128},{192,160},{224,1... | collective-permute-start | bytes 1536008 | tf_op jit(solution)/shard_map/ppermute | solution.py:309
  153.8 11.4 %collective-permute-start.7 = (bf16[1000,256]{1,0:T(8,128)(2,1)S(1)}, bf16[1000,256]{1,0:T(8,128)(2,1)S(1)}, u32[]{:S(2)}, u32[]{:S(2)}) collective-permute-start(bf16[1000,256]{1,0:T(8,128)(2,1)S(1)} %collective-permute-done.6.refs_6_), channel_id=1, source_target_pairs={{0,32},{32,64},{64,96},{96,128},{128,160},{160,192},{192,224},{224... | collective-permute-start | bytes 1536008 | tf_op jit(solution)/shard_map/ppermute | solution.py:307
  155.7 18.7 %collective-permute-start.15 = (bf16[1000,256]{1,0:T(8,128)(2,1)S(1)}, bf16[1000,256]{1,0:T(8,128)(2,1)S(1)}, u32[]{:S(2)}, u32[]{:S(2)}) collective-permute-start(bf16[1000,256]{1,0:T(8,128)(2,1)S(1)} %collective-permute-done.14.refs_7_), channel_id=1, source_target_pairs={{0,480},{32,0},{64,32},{96,64},{128,96},{160,128},{192,160},{224,1... | collective-permute-start | bytes 1536008 | tf_op jit(solution)/shard_map/ppermute | solution.py:309
  165.3 14.7 %collective-permute-start.8 = (bf16[1000,256]{1,0:T(8,128)(2,1)S(1)}, bf16[1000,256]{1,0:T(8,128)(2,1)S(1)}, u32[]{:S(2)}, u32[]{:S(2)}) collective-permute-start(bf16[1000,256]{1,0:T(8,128)(2,1)S(1)} %collective-permute-done.7.refs_8_), channel_id=1, source_target_pairs={{0,32},{32,64},{64,96},{96,128},{128,160},{160,192},{192,224},{224... | collective-permute-start | bytes 1536008 | tf_op jit(solution)/shard_map/ppermute | solution.py:307
  174.4 5.6 %copy-start.1 = (s32[896]{0:T(1024)S(1)}, s32[896]{0:T(1024)}, u32[]{:S(2)}) copy-start(s32[896]{0:T(1024)} %ids_ref.1) | copy-start | bytes 10756
  183.0 20.3 %all-to-all-start.1 = ((f32[32,4,896]{2,1,0:T(4,128)}), f32[32,4,896]{2,1,0:T(4,128)S(1)}, u32[]{:S(2)}, u32[]{:S(2)}) async-start(f32[32,4,896]{2,1,0:T(4,128)} %stats.1), calls=%async_computation.1 | async-start | bytes 917504 | tf_op jit(solution)/shard_map/all_to_all | solution.py:331
  204.6 18.7 %all-to-all-start.2 = ((f32[16,1,128]{2,1,0:T(1,128)}), f32[16,1,128]{2,1,0:T(1,128)S(1)}, u32[]{:S(2)}, u32[]{:S(2)}) async-start(f32[16,1,128]{2,1,0:T(1,128)} %broadcast_in_dim.17), calls=%async_computation.2 | async-start | bytes 16384 | tf_op jit(solution)/shard_map/all_to_all | solution.py:333
